TPU v7x, 512 devices: a whole 4x8x8 slice. The times are simulated.
512 devices in a mesh: leaf: 128 (over y, z, core), sub: 4 (over x).
Axes of the slice: x: 4, y: 8, z: 8, core: 2. Of those that a mesh axis runs over, the one named last changes fastest.
Arguments:
- field: float32 [64, 524288], P(None, ('leaf', 'sub')), may hold values from -6 to 6
- coords: float32 [3, 524288], P(None, ('leaf', 'sub')), may hold values from -6 to 6
- basis: float32 [2048, 64, 256], P(('leaf', 'sub')), may hold values from -0.375 to 0.375
- up_transfer: float32 [2048, 64, 64], P(('leaf', 'sub')), may hold values from -0.1875 to 0.1875
- down_transfer: float32 [2048, 64, 64], P(('leaf', 'sub')), may hold values from -0.75 to 0.75
- couplings: float32 [16384, 64, 64], P(('leaf', 'sub')), may hold values from -0.25 to 0.25
- top_coupling: float32 [128, 128, 64, 64], P('leaf', None, 'sub'), may hold values from -0.25 to 0.25
- send_leaf: int32 [128, 4, 128, 1], P('leaf', 'sub'), may hold values from 0 to 3
- list_slot: int32 [2048, 8], P(('leaf', 'sub')), may hold values from 0 to 127, as said below
- list_block: int32 [2048, 8], P(('leaf', 'sub')), may hold values from 0 to 31
Outputs:
- result: float32 [64, 524288], P(None, ('leaf', 'sub'))
Inputs may be any that keep to these rules, and one draw needn't show every extreme that they name: send_leaf[e, s, d, c] is the leaf, among the 4 of device (e, s), whose skeleton fills slot c of what that device sends to device (d, s). `list_slot`: a list entry q names slot q % 1 from the device q // 1 of the leaf axis with the same sub index; where a device's 4 * 8 list entries are at least 128, every slot is named by some entry of that device, else the device's entries are all different. `list_block`: a list entry names one of the 32 coupling blocks of the leaf's own device.
All inputs are finite; a program needn't handle non-finite values.
Results may differ from a plain program's by a relative error of at most 0.0001.
Values sent between devices are 32-bit elements; how exact they have to be, the bound alone decides.
A program may use at most 64 MiB of HBM per device.

v0:
```python
import math

import jax
import jax.numpy as jnp
from jax import lax
from jax.sharding import PartitionSpec as P

highest = lax.Precision.HIGHEST


def extended(block, sides, width):
    for axis, dim in sides:
        count = lax.axis_size(axis)
        forward = [(i, i + 1) for i in range(count - 1)]
        backward = [(target, source) for source, target in forward]
        low = lax.ppermute(
            lax.slice_in_dim(block, block.shape[dim] - width, None, axis=dim), axis, forward
        )
        high = lax.ppermute(lax.slice_in_dim(block, 0, width, axis=dim), axis, backward)
        block = jnp.concatenate([low, block, high], axis=dim)
    return block


def kernel_block(source_points, target_points, leaf_size):
    dist = jnp.zeros((source_points.shape[1], target_points.shape[1]), jnp.float32)
    for component in range(3):
        gap = source_points[component][:, None] - target_points[component][None, :]
        dist = dist + gap * gap
    return jnp.exp(-0.5 * dist) * (1.0 / math.sqrt(leaf_size))


def add_top(rows, coupling_rows):
    return jnp.einsum("epr,erq->pq", rows, coupling_rows, precision=highest)


def far_terms(incoming, list_slot, chosen, rows, rank):
    gathered = incoming.reshape(-1, rows, rank)[list_slot]
    return jnp.einsum("lkpr,lkrq->lpq", gathered, chosen, precision=highest)


def one_product(
    field,
    coords,
    basis,
    up_transfer,
    down_transfer,
    couplings,
    top_coupling,
    send_leaf,
    list_slot,
    list_block,
):
    rhs_count = field.shape[0]
    leaf_count = basis.shape[0]
    rank = basis.shape[1]
    leaf_size = basis.shape[2]
    stacked = jnp.concatenate([field, coords], 0)
    padded = extended(stacked, ((("leaf", "sub"), 1),), leaf_size)
    leaf_field = field.reshape(rhs_count, leaf_count, leaf_size)
    skeleton = jnp.einsum("pla,lra->lpr", leaf_field, basis, precision=highest)
    outgoing = skeleton[send_leaf.reshape(-1)]
    slot_total = outgoing.shape[0]
    chosen = couplings[list_block]
    incoming = lax.all_to_all(
        outgoing.reshape(slot_total, rhs_count * rank),
        "leaf",
        split_axis=0,
        concat_axis=0,
        tiled=True,
    )
    far = far_terms(incoming, list_slot, chosen, rhs_count, rank)

    def near_leaf(position):
        window = lax.dynamic_slice_in_dim(padded, position * leaf_size, 3 * leaf_size, 1)
        own_points = lax.dynamic_slice_in_dim(
            padded[rhs_count:], (position + 1) * leaf_size, leaf_size, 1
        )
        kernels = kernel_block(window[rhs_count:], own_points, leaf_size)
        return jnp.dot(
            window[:rhs_count], kernels, precision=highest, preferred_element_type=jnp.float32
        )

    near = lax.map(near_leaf, jnp.arange(leaf_count, dtype=jnp.int32))
    parent_part = jnp.einsum("lpr,lrq->pq", skeleton, up_transfer, precision=highest)
    quarter = top_coupling.shape[2]
    coupling_rows = top_coupling[0]
    parent = lax.psum(parent_part, "sub")
    row_start = lax.axis_index("sub") * quarter
    rows = lax.dynamic_slice_in_dim(
        lax.all_gather(parent[None], "leaf", axis=0, tiled=True), row_start, quarter, 2
    )
    top_partial = add_top(rows, coupling_rows)
    top_term = lax.psum(top_partial, "sub")
    coef = far + jnp.einsum("pr,lrq->lpq", top_term, down_transfer, precision=highest)
    total = near + jnp.einsum("lpr,lra->lpa", coef, basis, precision=highest)
    return total.transpose(1, 0, 2).reshape(rhs_count, leaf_count * leaf_size)


def local(
    field,
    coords,
    basis,
    up_transfer,
    down_transfer,
    couplings,
    top_coupling,
    send_leaf,
    list_slot,
    list_block,
):
    current = field
    for repeat in range(2):
        current = one_product(
            current,
            coords,
            basis,
            up_transfer,
            down_transfer,
            couplings,
            top_coupling,
            send_leaf,
            list_slot,
            list_block,
        )
    return current


def solution(mesh):
    in_specs = (
        P(None, ("leaf", "sub")),
        P(None, ("leaf", "sub")),
        P(("leaf", "sub"), None, None),
        P(("leaf", "sub"), None, None),
        P(("leaf", "sub"), None, None),
        P(("leaf", "sub"), None, None),
        P("leaf", None, "sub", None),
        P("leaf", "sub", None, None),
        P(("leaf", "sub"), None),
        P(("leaf", "sub"), None),
    )
    out_specs = P(None, ("leaf", "sub"))
    return jax.shard_map(local, mesh=mesh, in_specs=in_specs, out_specs=out_specs, check_vma=False)
```

profile of v0, /device:TPU:1, one launch (start us, length us, event | category | flops | bytes accessed | tf_op | source)
XLA Modules:
  0.0 376.9 jit_solution(1473924243727374704)
XLA Ops:
  6.5 1.5 fusion.52
  9.2 15.1 %psum.28 = f32[1,64,64]{2,1,0:T(8,128)} all-reduce(f32[1,64,64]{2,1,0:T(8,128)S(1)} %convolution_bitcast_fusion.9), channel_id=1, replica_groups=mesh['leaf'=128,'sub'=4] {'sub'}, use_global_device_ids=true, to_apply=%region_2.3 | all-reduce | flops 4096 | bytes 32768 | tf_op jit(solution)/shard_map/psum | solution.py:87
  25.6 2.8 gather_fusion
  28.4 3.8 %copy.27 = f32[128,64,64]{0,2,1:T(8,128)S(1)} copy(f32[128,64,64]{2,1,0:T(8,128)} %gather_fusion) | data formatting | bytes 4194304 | tf_op jit(solution)/shard_map/gather | solution.py:61
  32.2 4.1 %copy.28 = f32[128,1,4096]{2,1,0:T(1,128)} copy(f32[128,1,4096]{0,2,1:T(8,128)S(1)} %bitcast.122) | data formatting | bytes 4194304 | tf_op jit(solution)/shard_map/all_to_all | solution.py:64
  36.3 21.5 %all-to-all-start = ((f32[128,1,4096]{2,1,0:T(1,128)}), f32[128,1,4096]{2,1,0:T(1,128)}, u32[]{:S(2)}, u32[]{:S(2)}) async-start(f32[128,1,4096]{2,1,0:T(1,128)} %copy.28), calls=%async_computation | async-start | bytes 4194304 | tf_op jit(solution)/shard_map/all_to_all | solution.py:64
  57.9 1.9 collective-permute-start
  59.8 4.9 %collective-permute-start.1 = (f32[67,256]{1,0:T(8,128)S(1)}, f32[67,256]{1,0:T(8,128)S(1)}, u32[]{:S(2)}, u32[]{:S(2)}) collective-permute-start(f32[67,256]{1,0:T(8,128)S(1)} %get-tuple-element.82), channel_id=1, source_target_pairs={{1,0},{2,1},{3,2},{4,3},{5,4},{6,5},{7,6},{8,7},{9,8},{10,9},{11,1... | collective-permute-start | bytes 205832 | tf_op jit(solution)/shard_map/ppermute | solution.py:19
  66.2 11.9 %while.20 = (s32[]{:T(128)}, f32[4,64,256]{2,1,0:T(8,128)S(1)}, s32[4]{0:T(128)S(1)}, f32[67,1536]{1,0:T(8,128)S(1)}, s32[]{:T(128)}, /*index=5*/s32[1]{0:T(128)...) while((s32[]{:T(128)}, f32[4,64,256]{2,1,0:T(8,128)S(1)}, ...), condition=%wide.region_1.2_spmd, body=%wide.region_0.1_spmd.sunk | while | flops 152961040 | bytes 339289 | solution.py:83
  78.2 73.1 %all-gather.3.cloned.1.call-done = f32[128,64,64]{2,1,0:T(8,128)} async-done(((f32[1,64,64]{2,1,0:T(8,128)}), f32[128,64,64]{2,1,0:T(8,128)}) %all-gather.3.cloned.1.call-update) | async-done | bytes 2097168 | tf_op jit(solution)/shard_map/all_gather | solution.py:90
  151.3 5.3 %constant_dynamic-slice_fusion.3 = f32[128,64,16]{2,1,0:T(8,128)} fusion(f32[128,64,64]{2,1,0:T(8,128)} %all-gather.3.cloned.1.call-done, s32[]{:T(128)S(6)} %select_n.38), kind=kLoop, calls=%fused_computation.99 | loop fusion | bytes 1048580 | tf_op jit(solution)/shard_map/dynamic_slice | solution.py:89
  156.6 4.0 %copy.41 = f32[128,64,16]{0,1,2:T(8,128)S(1)} copy(f32[128,64,16]{2,1,0:T(8,128)} %constant_dynamic-slice_fusion.3) | data formatting | bytes 1048576
  161.2 13.8 %psum.29 = f32[64,64]{1,0:T(8,128)} all-reduce(f32[64,64]{1,0:T(8,128)S(1)} %convolution_bitcast_fusion.8), channel_id=1, replica_groups=mesh['leaf'=128,'sub'=4] {'sub'}, use_global_device_ids=true, to_apply=%region_3.4 | all-reduce | flops 4096 | bytes 32768 | tf_op jit(solution)/shard_map/psum | solution.py:93
  175.0 5.6 %copy.29 = f32[128,1,4096]{0,2,1:T(8,128)} copy(f32[128,1,4096]{2,1,0:T(1,128)} %all-to-all-done) | data formatting | bytes 4194304 | tf_op jit(solution)/shard_map/all_to_all | solution.py:64
  180.7 5.6 %copy.30 = f32[128,64,64]{2,1,0:T(8,128)} copy(f32[128,64,64]{0,2,1:T(8,128)} %bitcast.123) | data formatting | bytes 4194304 | tf_op jit(solution)/shard_map/reshape | solution.py:37
  186.3 2.9 gather_fusion.1
  191.7 1.3 fusion.55
  194.3 11.6 %psum.30 = f32[1,64,64]{2,1,0:T(8,128)} all-reduce(f32[1,64,64]{2,1,0:T(8,128)S(1)} %convolution_bitcast_fusion.7), channel_id=1, replica_groups=mesh['leaf'=128,'sub'=4] {'sub'}, use_global_device_ids=true, to_apply=%region_6.7 | all-reduce | flops 4096 | bytes 32768 | tf_op jit(solution)/shard_map/psum | solution.py:87
  205.8 2.9 gather_fusion.3
  208.8 4.7 %copy.33 = f32[128,64,64]{0,2,1:T(8,128)} copy(f32[128,64,64]{2,1,0:T(8,128)} %gather_fusion.3) | data formatting | bytes 4194304 | tf_op jit(solution)/shard_map/gather | solution.py:61
  213.5 5.7 %copy.34 = f32[128,1,4096]{2,1,0:T(1,128)} copy(f32[128,1,4096]{0,2,1:T(8,128)} %bitcast.124) | data formatting | bytes 4194304 | tf_op jit(solution)/shard_map/all_to_all | solution.py:64
  219.2 17.1 %all-to-all-start.1 = ((f32[128,1,4096]{2,1,0:T(1,128)}), f32[128,1,4096]{2,1,0:T(1,128)}, u32[]{:S(2)}, u32[]{:S(2)}) async-start(f32[128,1,4096]{2,1,0:T(1,128)} %copy.34), calls=%async_computation.1 | async-start | bytes 4194304 | tf_op jit(solution)/shard_map/all_to_all | solution.py:64
  236.4 2.3 collective-permute-start.2
  238.8 4.4 %collective-permute-start.3 = (f32[67,256]{1,0:T(8,128)S(1)}, f32[67,256]{1,0:T(8,128)S(1)}, u32[]{:S(2)}, u32[]{:S(2)}) collective-permute-start(f32[67,256]{1,0:T(8,128)S(1)} %get-tuple-element.80), channel_id=1, source_target_pairs={{1,0},{2,1},{3,2},{4,3},{5,4},{6,5},{7,6},{8,7},{9,8},{10,9},{11,1... | collective-permute-start | bytes 205832 | tf_op jit(solution)/shard_map/ppermute | solution.py:19
  244.7 11.9 %while.21 = (s32[]{:T(128)}, f32[4,64,256]{2,1,0:T(8,128)S(1)}, s32[4]{0:T(128)S(1)}, f32[67,1536]{1,0:T(8,128)S(1)}, s32[]{:T(128)}, /*index=5*/s32[1]{0:T(128)...) while((s32[]{:T(128)}, f32[4,64,256]{2,1,0:T(8,128)S(1)}, ...), condition=%wide.region_5.6_spmd, body=%wide.region_4.5_spmd.sunk | while | flops 152961040 | bytes 339289 | solution.py:83
  256.6 71.4 %all-gather.5.cloned.1.call-done = f32[128,64,64]{2,1,0:T(8,128)} async-done(((f32[1,64,64]{2,1,0:T(8,128)}), f32[128,64,64]{2,1,0:T(8,128)}) %all-gather.5.cloned.1.call-update) | async-done | bytes 2097168 | tf_op jit(solution)/shard_map/all_gather | solution.py:90
  328.1 5.3 %constant_dynamic-slice_fusion.2 = f32[128,64,16]{2,1,0:T(8,128)} fusion(f32[128,64,64]{2,1,0:T(8,128)} %all-gather.5.cloned.1.call-done, s32[]{:T(128)S(6)} %select_n.38), kind=kLoop, calls=%fused_computation.98 | loop fusion | bytes 1048580 | tf_op jit(solution)/shard_map/dynamic_slice | solution.py:89
  333.4 4.0 %copy.42 = f32[128,64,16]{0,1,2:T(8,128)S(1)} copy(f32[128,64,16]{2,1,0:T(8,128)} %constant_dynamic-slice_fusion.2) | data formatting | bytes 1048576
  338.0 13.8 %psum.31 = f32[64,64]{1,0:T(8,128)} all-reduce(f32[64,64]{1,0:T(8,128)S(1)} %convolution_bitcast_fusion.6), channel_id=1, replica_groups=mesh['leaf'=128,'sub'=4] {'sub'}, use_global_device_ids=true, to_apply=%region_7.8 | all-reduce | flops 4096 | bytes 32768 | tf_op jit(solution)/shard_map/psum | solution.py:93
  351.8 5.6 %copy.35 = f32[128,1,4096]{0,2,1:T(8,128)} copy(f32[128,1,4096]{2,1,0:T(1,128)} %all-to-all-done.1) | data formatting | bytes 4194304 | tf_op jit(solution)/shard_map/all_to_all | solution.py:64
  357.5 5.6 %copy.36 = f32[128,64,64]{2,1,0:T(8,128)} copy(f32[128,64,64]{0,2,1:T(8,128)} %bitcast.125) | data formatting | bytes 4194304 | tf_op jit(solution)/shard_map/reshape | solution.py:37
  363.1 2.8 gather_fusion.4
  (114 shorter events, 28.2 us)
Async XLA Ops:
  6.5 58.9 %copy-start = (f32[32,64,64]{2,1,0:T(8,128)S(1)}, f32[32,64,64]{2,1,0:T(8,128)}, u32[]{:S(2)}) copy-start(f32[32,64,64]{2,1,0:T(8,128)} %param.19) | copy-start | bytes 1572868
  6.5 144.7 %all-gather.3.cloned.1.call-start = ((), (), s32[]{:S(2)}) async-start(), calls=%async_computation.2 | async-start | bytes 4227072 | tf_op jit(solution)/shard_map/all_gather | solution.py:90
  25.0 0.6 copy-start.12
  32.2 25.6 %copy-start.7 = (f32[64,1024]{1,0:T(8,128)S(1)}, f32[64,1024]{1,0:T(8,128)}, u32[]{:S(2)}) copy-start(f32[64,1024]{1,0:T(8,128)} %param.14) | copy-start | bytes 786436
  32.2 25.7 %copy-start.10 = (f32[3,1024]{1,0:T(4,128)S(1)}, f32[3,1024]{1,0:T(4,128)}, u32[]{:S(2)}) copy-start(f32[3,1024]{1,0:T(4,128)} %param.15) | copy-start | bytes 36868
  32.2 32.5 %copy-start.13 = (s32[4,8]{1,0:T(4,128)S(1)}, s32[4,8]{1,0:T(4,128)}, u32[]{:S(2)}) copy-start(s32[4,8]{1,0:T(4,128)} %param.22) | copy-start | bytes 388
  32.2 32.6 %copy-start.14 = (s32[4,8]{1,0:T(4,128)S(1)}, s32[4,8]{1,0:T(4,128)}, u32[]{:S(2)}) copy-start(s32[4,8]{1,0:T(4,128)} %param.23) | copy-start | bytes 388
  36.3 138.7 %all-to-all-start = ((f32[128,1,4096]{2,1,0:T(1,128)}), f32[128,1,4096]{2,1,0:T(1,128)}, u32[]{:S(2)}, u32[]{:S(2)}) async-start(f32[128,1,4096]{2,1,0:T(1,128)} %copy.28), calls=%async_computation | async-start | bytes 4194304 | tf_op jit(solution)/shard_map/all_to_all | solution.py:64
  57.8 270.3 %all-gather.5.cloned.1.call-start = ((), (), s32[]{:S(2)}) async-start(), calls=%async_computation.3 | async-start | bytes 4227072 | tf_op jit(solution)/shard_map/all_gather | solution.py:90
  57.9 8.2 %collective-permute-start = (f32[67,256]{1,0:T(8,128)S(1)}, f32[67,256]{1,0:T(8,128)S(1)}, u32[]{:S(2)}, u32[]{:S(2)}) collective-permute-start(f32[67,256]{1,0:T(8,128)S(1)} %get-tuple-element.81), channel_id=1, source_target_pairs={{0,1},{1,2},{2,3},{3,4},{4,5},{5,6},{6,7},{7,8},{8,9},{9,10},{10,1... | collective-permute-start | bytes 205832 | tf_op jit(solution)/shard_map/ppermute | solution.py:16
  59.8 6.3 %collective-permute-start.1 = (f32[67,256]{1,0:T(8,128)S(1)}, f32[67,256]{1,0:T(8,128)S(1)}, u32[]{:S(2)}, u32[]{:S(2)}) collective-permute-start(f32[67,256]{1,0:T(8,128)S(1)} %get-tuple-element.82), channel_id=1, source_target_pairs={{1,0},{2,1},{3,2},{4,3},{5,4},{6,5},{7,6},{8,7},{9,8},{10,9},{11,1... | collective-permute-start | bytes 205832 | tf_op jit(solution)/shard_map/ppermute | solution.py:19
  78.2 78.4 %copy-start.2 = (f32[4,64,256]{2,1,0:T(8,128)}, f32[4,64,256]{2,1,0:T(8,128)S(1)}, u32[]{:S(2)}) copy-start(f32[4,64,256]{2,1,0:T(8,128)S(1)} %get-tuple-element.49) | copy-start | bytes 786436
  156.6 4.0 %copy-start.4 = (f32[1,128,16,64]{1,3,2,0:T(8,128)S(1)}, f32[1,128,16,64]{1,3,2,0:T(8,128)}, u32[]{:S(2)}) copy-start(f32[1,128,16,64]{1,3,2,0:T(8,128)} %param.20) | copy-start | bytes 1572868
  180.7 9.7 %copy-start.8 = (f32[4,64,64]{2,1,0:T(8,128)S(1)}, f32[4,64,64]{2,1,0:T(8,128)}, u32[]{:S(2)}) copy-start(f32[4,64,64]{2,1,0:T(8,128)} %param.18) | copy-start | bytes 196612
  180.7 10.7 %copy-start.1 = (f32[4,64,256]{2,1,0:T(8,128)S(1)}, f32[4,64,256]{2,1,0:T(8,128)}, u32[]{:S(2)}) copy-start(f32[4,64,256]{2,1,0:T(8,128)} %param.16) | copy-start | bytes 786436
  213.5 22.8 %copy-start.3 = (f32[4,64,256]{2,1,0:T(8,128)S(1)}, f32[4,64,256]{2,1,0:T(8,128)}, u32[]{:S(2)}) copy-start(f32[4,64,256]{2,1,0:T(8,128)} %copy-done.2) | copy-start | bytes 786436
  219.2 132.6 %all-to-all-start.1 = ((f32[128,1,4096]{2,1,0:T(1,128)}), f32[128,1,4096]{2,1,0:T(1,128)}, u32[]{:S(2)}, u32[]{:S(2)}) async-start(f32[128,1,4096]{2,1,0:T(1,128)} %copy.34), calls=%async_computation.1 | async-start | bytes 4194304 | tf_op jit(solution)/shard_map/all_to_all | solution.py:64
  236.4 7.3 %collective-permute-start.2 = (f32[67,256]{1,0:T(8,128)S(1)}, f32[67,256]{1,0:T(8,128)S(1)}, u32[]{:S(2)}, u32[]{:S(2)}) collective-permute-start(f32[67,256]{1,0:T(8,128)S(1)} %get-tuple-element.79), channel_id=1, source_target_pairs={{0,1},{1,2},{2,3},{3,4},{4,5},{5,6},{6,7},{7,8},{8,9},{9,10},{10,1... | collective-permute-start | bytes 205832 | tf_op jit(solution)/shard_map/ppermute | solution.py:16
  238.8 5.8 %collective-permute-start.3 = (f32[67,256]{1,0:T(8,128)S(1)}, f32[67,256]{1,0:T(8,128)S(1)}, u32[]{:S(2)}, u32[]{:S(2)}) collective-permute-start(f32[67,256]{1,0:T(8,128)S(1)} %get-tuple-element.80), channel_id=1, source_target_pairs={{1,0},{2,1},{3,2},{4,3},{5,4},{6,5},{7,6},{8,7},{9,8},{10,9},{11,1... | collective-permute-start | bytes 205832 | tf_op jit(solution)/shard_map/ppermute | solution.py:19
  256.6 71.5 %copy-start.6 = (f32[4,64,256]{2,1,0:T(8,128)}, f32[4,64,256]{2,1,0:T(8,128)S(1)}, u32[]{:S(2)}) copy-start(f32[4,64,256]{2,1,0:T(8,128)S(1)} %get-tuple-element.50) | copy-start | bytes 786436
  333.4 4.0 %copy-start.5 = (f32[1,128,16,64]{1,3,2,0:T(8,128)S(1)}, f32[1,128,16,64]{1,3,2,0:T(8,128)}, u32[]{:S(2)}) copy-start(f32[1,128,16,64]{1,3,2,0:T(8,128)} %param.20) | copy-start | bytes 1572868
  357.5 5.6 %copy-start.11 = (s32[1024]{0:T(1024)S(1)}, s32[1024]{0:T(1024)}, u32[]{:S(2)}) copy-start(s32[1024]{0:T(1024)} %get-tuple-element.84) | copy-start | bytes 12292
  357.5 9.5 %copy-start.9 = (f32[4,64,64]{2,1,0:T(8,128)S(1)}, f32[4,64,64]{2,1,0:T(8,128)}, u32[]{:S(2)}) copy-start(f32[4,64,64]{2,1,0:T(8,128)} %param.18) | copy-start | bytes 196612
Sparse Core Ops, SparseCore 0:
  24.5 126.7 all-gather.2
  206.0 122.0 all-gather.4
where the time goes:
time: 381 us; the launch traced here: 377 us
  waiting for transfers between devices  146 us (38%)
  local copies, waits for them, and re-layouts  79.5 us (21%)
  blocking collectives  54.3 us (14%)
  starting transfers between devices  52.1 us (14%)
  matrix products  18.6 us (5%)
  between operations  13.9 us (4%)
  loops' own time  10.3 us (3%)
    all_gather x2, waiting for transfers between devices, one_product(): lax.all_gather(parent[None], 'leaf', axis=0, tiled=True)  145 us
    all_to_all x2, starting transfers between devices, one_product(): lax.all_to_all(outgoing.reshape(slot_total, rhs_count * rank), 'leaf', sp...  38.5 us
    psum x2, blocking collectives, one_product(): top_term = lax.psum(top_partial, 'sub')  27.7 us
    psum x2, blocking collectives, one_product(): parent = lax.psum(parent_part, 'sub')  26.6 us
    all_to_all x4, local copies, waits for them, and re-layouts, one_product(): lax.all_to_all(outgoing.reshape(slot_total, rhs_count * rank), 'leaf', sp...  21 us
    gather x4, local copies, waits for them, and re-layouts, one_product(): outgoing = skeleton[send_leaf.reshape(-1)]  14.2 us
    reshape x2, local copies, waits for them, and re-layouts, far_terms(): gathered = incoming.reshape(-1, rows, rank)[list_slot]  11.2 us
    dynamic_slice x2, local copies, waits for them, and re-layouts, one_product(): lax.dynamic_slice_in_dim(lax.all_gather(parent[None], 'leaf', axis=0, til...  10.6 us
  transfers between devices with their start and end apart: 8, of which 4 were waited for; matrix products, arithmetic and copies ran while one was open for 16% of the time, Pallas kernels for 0%

commit v1 on v0

v1 whole, which is shorter than its diff:
```python
import math

import jax
import jax.numpy as jnp
from jax import lax
from jax.sharding import PartitionSpec as P

precise = lax.Precision.HIGH


def halo(block, axes, count):
    forward = [(i, i + 1) for i in range(count - 1)]
    backward = [(target, source) for source, target in forward]
    low = lax.ppermute(block[:, -1], axes, forward)
    high = lax.ppermute(block[:, 0], axes, backward)
    return jnp.concatenate([low[:, None], block, high[:, None]], axis=1)


def shifted(values, axis, count, step):
    return lax.ppermute(values, axis, [(i, (i + step) % count) for i in range(count)])


def kernel_blocks(sources, targets, leaf_size):
    dist = 0.0
    for component in range(3):
        gap = sources[component][:, :, None] - targets[component][:, None, :]
        dist = dist + gap * gap
    return jnp.exp(-0.5 * dist) * (1.0 / math.sqrt(leaf_size))


def fold(values):
    half = values.shape[-2] // 2
    return jnp.concatenate([values[..., :half, :], values[..., half:, :]], axis=-1)


def unfold(values):
    half = values.shape[-1] // 2
    return jnp.concatenate([values[..., :half], values[..., half:]], axis=-2)


def one_product(field, near_kernels, basis, up, down, couplings, top, send, slots, blocks):
    rhs, leaves, size = field.shape
    rank = basis.shape[1]
    subs = lax.axis_size("sub")
    quarter = rank // subs
    sub = lax.axis_index("sub")
    count = lax.axis_size("leaf") * subs
    skeleton = jnp.einsum("pla,lra->lpr", field, basis, precision=precise)
    parent_t = jnp.einsum("lpr,lrq->qp", skeleton, up, precision=precise)
    parts = parent_t.reshape(subs, quarter, rhs)
    own = lax.dynamic_index_in_dim(parts, sub, 0, keepdims=False)
    for step in range(1, subs):
        piece = lax.dynamic_index_in_dim(parts, (sub + step) % subs, 0, keepdims=False)
        own = own + shifted(piece, "sub", subs, step)
    packed = fold(skeleton)[send]
    rows = packed.shape[1]
    parent = jnp.broadcast_to(fold(own)[None], (packed.shape[0], quarter // 2, 2 * rhs))
    outgoing = jnp.concatenate([packed, parent], axis=1)
    incoming = lax.all_to_all(outgoing, "leaf", split_axis=0, concat_axis=0, tiled=True)
    padded = halo(field, ("leaf", "sub"), count)
    near = 0.0
    for side in range(3):
        near = near + jnp.einsum(
            "plb,lba->pla", padded[:, side : side + leaves], near_kernels[side], precision=precise
        )
    parents = unfold(incoming[:, rows:])
    top_part = jnp.einsum("erp,erq->pq", parents, top, precision=precise)
    folded = fold(top_part)
    summed = folded
    for step in range(1, subs):
        summed = summed + shifted(folded, "sub", subs, step)
    top_term = unfold(summed)
    gathered = unfold(incoming[slots][:, :, :rows])
    far = jnp.einsum("lkpr,lkrq->lpq", gathered, couplings[blocks], precision=precise)
    coef = far + jnp.einsum("pr,lrq->lpq", top_term, down, precision=precise)
    return near + jnp.einsum("lpr,lra->pla", coef, basis, precision=precise)


def local(
    field, coords, basis, up_transfer, down_transfer, couplings, top_coupling, send_leaf, list_slot, list_block
):
    rhs = field.shape[0]
    leaves, _, size = basis.shape
    count = lax.axis_size("leaf") * lax.axis_size("sub")
    points = coords.reshape(3, leaves, size)
    all_points = halo(points, ("leaf", "sub"), count)
    near_kernels = [
        kernel_blocks(all_points[:, side : side + leaves], points, size) for side in range(3)
    ]
    current = field.reshape(rhs, leaves, size)
    for repeat in range(2):
        current = one_product(
            current,
            near_kernels,
            basis,
            up_transfer,
            down_transfer,
            couplings,
            top_coupling[0],
            send_leaf.reshape(-1),
            list_slot,
            list_block,
        )
    return current.reshape(rhs, leaves * size)


def solution(mesh):
    joined = ("leaf", "sub")
    in_specs = (
        P(None, joined),
        P(None, joined),
        P(joined, None, None),
        P(joined, None, None),
        P(joined, None, None),
        P(joined, None, None),
        P("leaf", None, "sub", None),
        P("leaf", "sub", None, None),
        P(joined, None),
        P(joined, None),
    )
    return jax.shard_map(local, mesh=mesh, in_specs=in_specs, out_specs=P(None, joined), check_vma=False)
```

time: 381 us -> 228 us (0.60)
  local copies, waits for them, and re-layouts: 79.5 us -> 13.6 us
  blocking collectives: 54.3 us -> 0 us
  waiting for transfers between devices: 146 us -> 96.4 us
  starting transfers between devices: 52.1 us -> 93.3 us
  between operations: 13.9 us -> 0.99 us
  loops' own time: 10.3 us -> 0 us
  other arithmetic: 2.35 us -> 7.66 us
    all_gather x2 -> x0, waiting for transfers between devices: 145 us -> none  [one_product(): lax.all_gather(parent[None], 'leaf', axis=0, tiled=True)]
    all_to_all x2, waiting for transfers between devices: 0.01 us -> 90.5 us  [one_product(): lax.all_to_all(outgoing, 'leaf', split_axis=0, concat_axis=0, tiled=True)]
    psum x4 -> x0, blocking collectives: 54.3 us -> none  [the longest x2 27.7 us: one_product(): top_term = lax.psum(top_partial, 'sub')]
    ppermute x4 -> x18, starting transfers between devices: 13.5 us -> 59.4 us  [the longest x12 39.5 us: shifted(): lax.ppermute(values, axis, [(i, (i + step) % count) for i in range(count)])]
    all_to_all x4 -> x0, local copies, waits for them, and re-layouts: 21 us -> none  [one_product(): lax.all_to_all(outgoing.reshape(slot_total, rhs_count * rank), 'leaf', sp...]
    dynamic_slice x10 -> x0, local copies, waits for them, and re-layouts: 15.4 us -> none  [the longest x2 10.6 us: one_product(): lax.dynamic_slice_in_dim(lax.all_gather(parent[None], 'leaf', axis=0, til...]
    gather x7 -> x5, local copies, waits for them, and re-layouts: 20.6 us -> 8.32 us  [the longest x2 4.66 us: one_product(): gathered = unfold(incoming[slots][:, :, :rows])]
    reshape x4 -> x3, local copies, waits for them, and re-layouts: 12 us -> 0.76 us  [the longest x1 0.72 us: local(): return current.reshape(rhs, leaves * size)]
  transfers between devices with their start and end apart: 8 -> 20, of which waited for: 4 -> 4; matrix products, arithmetic and copies ran while one was open for 16% -> 8% of each run, Pallas kernels for 0% -> 0%
where the time goes in v1:
time: 228 us; the launch traced here: 227 us
  waiting for transfers between devices  96.4 us (42%)
  starting transfers between devices  93.3 us (41%)
  matrix products  14.9 us (7%)
  local copies, waits for them, and re-layouts  13.6 us (6%)
  other arithmetic  7.66 us (3%)
    all_to_all x2, waiting for transfers between devices, one_product(): lax.all_to_all(outgoing, 'leaf', split_axis=0, concat_axis=0, tiled=True)  90.5 us
    ppermute x12, starting transfers between devices, shifted(): lax.ppermute(values, axis, [(i, (i + step) % count) for i in range(count)])  39.5 us
    all_to_all x2, starting transfers between devices, one_product(): lax.all_to_all(outgoing, 'leaf', split_axis=0, concat_axis=0, tiled=True)  34 us
    ppermute x3, starting transfers between devices, halo(): high = lax.ppermute(block[:, 0], axes, backward)  14.2 us
    dot_general x6, matrix products, one_product(): jnp.einsum('plb,lba->pla', padded[:, side:side + leaves], near_kernels[si...  6.6 us
    ppermute x3, waiting for transfers between devices, halo(): low = lax.ppermute(block[:, -1], axes, forward)  5.85 us
    ppermute x3, starting transfers between devices, halo(): low = lax.ppermute(block[:, -1], axes, forward)  5.76 us
    concatenate x2, other arithmetic, one_product(): outgoing = jnp.concatenate([packed, parent], axis=1)  4.97 us
  transfers between devices with their start and end apart: 20, of which 4 were waited for; matrix products, arithmetic and copies ran while one was open for 8% of the time, Pallas kernels for 0%

profile of v1, /device:TPU:1, one launch (start us, length us, event | category | flops | bytes accessed | tf_op | source)
XLA Modules:
  0.0 226.9 jit_solution(6403233412699704753)
XLA Ops:
  2.6 3.9 %collective-permute-start.4 = (f32[16,64]{1,0:T(8,128)S(1)}, f32[16,64]{1,0:T(8,128)S(1)}, u32[]{:S(2)}, u32[]{:S(2)}) collective-permute-start(f32[16,64]{1,0:T(8,128)S(1)} %get-tuple-element.31), channel_id=1, source_target_pairs={{0,1},{1,2},{2,3},{3,0},{4,5},{5,6},{6,7},{7,4},{8,9},{9,10},{10,1... | collective-permute-start | bytes 12296 | tf_op jit(solution)/shard_map/ppermute | solution.py:20
  6.6 4.4 %collective-permute-start.5 = (f32[16,64]{1,0:T(8,128)S(1)}, f32[16,64]{1,0:T(8,128)S(1)}, u32[]{:S(2)}, u32[]{:S(2)}) collective-permute-start(f32[16,64]{1,0:T(8,128)S(1)} %get-tuple-element.33), channel_id=1, source_target_pairs={{0,2},{1,3},{2,0},{3,1},{4,6},{5,7},{6,4},{7,5},{8,10},{9,11},{10,... | collective-permute-start | bytes 12296 | tf_op jit(solution)/shard_map/ppermute | solution.py:20
  10.9 3.1 %collective-permute-start.6 = (f32[16,64]{1,0:T(8,128)S(1)}, f32[16,64]{1,0:T(8,128)S(1)}, u32[]{:S(2)}, u32[]{:S(2)}) collective-permute-start(f32[16,64]{1,0:T(8,128)S(1)} %get-tuple-element.32), channel_id=1, source_target_pairs={{0,3},{1,0},{2,1},{3,2},{4,7},{5,4},{6,5},{7,6},{8,11},{9,8},{10,9... | collective-permute-start | bytes 12296 | tf_op jit(solution)/shard_map/ppermute | solution.py:20
  15.8 1.7 pad_maximum_fusion
  17.5 19.5 %all-to-all-start = ((f32[128,40,128]{2,1,0:T(8,128)}), f32[128,40,128]{2,1,0:T(8,128)}, u32[]{:S(2)}, u32[]{:S(2)}) async-start(f32[128,40,128]{2,1,0:T(8,128)} %pad_maximum_fusion), calls=%async_computation | async-start | bytes 5242880 | tf_op jit(solution)/shard_map/all_to_all | solution.py:59
  37.1 1.9 collective-permute-start
  39.0 5.1 %collective-permute-start.2 = (f32[3,256]{1,0:T(4,128)S(1)}, f32[3,256]{1,0:T(4,128)S(1)}, u32[]{:S(2)}, u32[]{:S(2)}) collective-permute-start(f32[3,256]{1,0:T(4,128)S(1)} %get-tuple-element.39), channel_id=1, source_target_pairs={{1,0},{2,1},{3,2},{4,3},{5,4},{6,5},{7,6},{8,7},{9,8},{10,9},{11,1... | collective-permute-start | bytes 9224 | tf_op jit(solution)/shard_map/ppermute | solution.py:15
  44.2 3.9 %collective-permute-start.3 = (f32[64,256]{1,0:T(8,128)S(1)}, f32[64,256]{1,0:T(8,128)S(1)}, u32[]{:S(2)}, u32[]{:S(2)}) collective-permute-start(f32[64,256]{1,0:T(8,128)S(1)} %get-tuple-element.19), channel_id=1, source_target_pairs={{1,0},{2,1},{3,2},{4,3},{5,4},{6,5},{7,6},{8,7},{9,8},{10,9},{11,1... | collective-permute-start | bytes 196616 | tf_op jit(solution)/shard_map/ppermute | solution.py:15
  48.1 1.9 collective-permute-start.1
  53.8 1.5 collective-permute-done.1
  55.4 1.6 fusion.6
  57.0 42.5 %all-to-all-done = f32[128,40,128]{2,1,0:T(8,128)} async-done(((f32[128,40,128]{2,1,0:T(8,128)}), f32[128,40,128]{2,1,0:T(8,128)}, u32[]{:S(2)}, u32[]{:S(2)}) %all-to-all-start) | async-done | bytes 2621472 | tf_op jit(solution)/shard_map/all_to_all | solution.py:59
  99.5 1.6 fusion.108
  102.4 1.9 collective-permute-start.7
  104.3 5.4 %collective-permute-start.8 = (f32[32,128]{1,0:T(8,128)S(1)}, f32[32,128]{1,0:T(8,128)}, u32[]{:S(2)}, u32[]{:S(2)}) collective-permute-start(f32[32,128]{1,0:T(8,128)S(1)} %pad_maximum_fusion.14), channel_id=1, source_target_pairs={{0,2},{1,3},{2,0},{3,1},{4,6},{5,7},{6,4},{7,5},{8,10},{9,11},{10,... | collective-permute-start | bytes 49160 | tf_op jit(solution)/shard_map/ppermute | solution.py:20
  109.8 1.9 collective-permute-start.9
  111.7 2.3 %gather_fusion.1 = f32[32,40,128]{2,1,0:T(8,128)S(1)} fusion(f32[128,40,128]{2,1,0:T(8,128)} %all-to-all-done, s32[1024]{0:T(1024)S(1)} %copy-done.10), kind=kCustom, calls=%fused_computation.1 | custom fusion | bytes 1310848 | tf_op jit(solution)/shard_map/gather | solution.py:73
  117.9 3.4 %collective-permute-start.12 = (f32[16,64]{1,0:T(8,128)S(1)}, f32[16,64]{1,0:T(8,128)S(1)}, u32[]{:S(2)}, u32[]{:S(2)}) collective-permute-start(f32[16,64]{1,0:T(8,128)S(1)} %get-tuple-element.26), channel_id=1, source_target_pairs={{0,1},{1,2},{2,3},{3,0},{4,5},{5,6},{6,7},{7,4},{8,9},{9,10},{10,1... | collective-permute-start | bytes 12296 | tf_op jit(solution)/shard_map/ppermute | solution.py:20
  121.3 2.2 collective-permute-start.13
  123.5 4.0 %collective-permute-start.14 = (f32[16,64]{1,0:T(8,128)S(1)}, f32[16,64]{1,0:T(8,128)S(1)}, u32[]{:S(2)}, u32[]{:S(2)}) collective-permute-start(f32[16,64]{1,0:T(8,128)S(1)} %get-tuple-element.27), channel_id=1, source_target_pairs={{0,3},{1,0},{2,1},{3,2},{4,7},{5,4},{6,5},{7,6},{8,11},{9,8},{10,9... | collective-permute-start | bytes 12296 | tf_op jit(solution)/shard_map/ppermute | solution.py:20
  127.6 2.2 gather_fusion.3
  130.0 3.3 %pad_maximum_fusion.1 = f32[128,40,128]{2,1,0:T(8,128)} fusion(f32[128,8,128]{2,1,0:T(8,128)S(1)} %broadcast_in_dim.49, f32[128,32,128]{2,1,0:T(8,128)} %gather_fusion.3), kind=kLoop, calls=%fused_computation.6 | loop fusion | flops 655360 | bytes 5242880 | tf_op jit(solution)/shard_map/concatenate | solution.py:58
  133.3 14.4 %all-to-all-start.1 = ((f32[128,40,128]{2,1,0:T(8,128)}), f32[128,40,128]{2,1,0:T(8,128)}, u32[]{:S(2)}, u32[]{:S(2)}) async-start(f32[128,40,128]{2,1,0:T(8,128)} %pad_maximum_fusion.1), calls=%async_computation.1 | async-start | bytes 5242880 | tf_op jit(solution)/shard_map/all_to_all | solution.py:59
  147.8 5.1 %collective-permute-start.11 = (f32[64,256]{1,0:T(8,128)S(1)}, f32[64,256]{1,0:T(8,128)S(1)}, u32[]{:S(2)}, u32[]{:S(2)}) collective-permute-start(f32[64,256]{1,0:T(8,128)S(1)} %get-tuple-element.17), channel_id=1, source_target_pairs={{1,0},{2,1},{3,2},{4,3},{5,4},{6,5},{7,6},{8,7},{9,8},{10,9},{11,1... | collective-permute-start | bytes 196616 | tf_op jit(solution)/shard_map/ppermute | solution.py:15
  154.1 1.9 collective-permute-start.10
  157.0 4.3 %collective-permute-done.10 = f32[64,256]{1,0:T(8,128)S(1)} collective-permute-done((f32[64,256]{1,0:T(8,128)S(1)}, f32[64,256]{1,0:T(8,128)S(1)}, u32[]{:S(2)}, u32[]{:S(2)}) %collective-permute-start.10) | collective-permute-done | bytes 65568 | tf_op jit(solution)/shard_map/ppermute | solution.py:14
  162.2 48.0 %all-to-all-done.1 = f32[128,40,128]{2,1,0:T(8,128)} async-done(((f32[128,40,128]{2,1,0:T(8,128)}), f32[128,40,128]{2,1,0:T(8,128)}, u32[]{:S(2)}, u32[]{:S(2)}) %all-to-all-start.1) | async-done | bytes 2621472 | tf_op jit(solution)/shard_map/all_to_all | solution.py:59
  210.2 1.6 fusion.107
  213.1 2.0 collective-permute-start.15
  215.2 5.3 %collective-permute-start.16 = (f32[32,128]{1,0:T(8,128)S(1)}, f32[32,128]{1,0:T(8,128)S(1)}, u32[]{:S(2)}, u32[]{:S(2)}) collective-permute-start(f32[32,128]{1,0:T(8,128)S(1)} %pad_maximum_fusion.15), channel_id=1, source_target_pairs={{0,2},{1,3},{2,0},{3,1},{4,6},{5,7},{6,4},{7,5},{8,10},{9,11},{10,... | collective-permute-start | bytes 49160 | tf_op jit(solution)/shard_map/ppermute | solution.py:20
  220.4 1.9 collective-permute-start.17
  222.4 2.3 %gather_fusion.4 = f32[32,40,128]{2,1,0:T(8,128)S(1)} fusion(f32[128,40,128]{2,1,0:T(8,128)} %all-to-all-done.1, s32[1024]{0:T(1024)S(1)} %copy-done.11), kind=kCustom, calls=%fused_computation.4 | custom fusion | bytes 1310848 | tf_op jit(solution)/shard_map/gather | solution.py:73
  (149 shorter events, 19.5 us)
Async XLA Ops:
  0.0 52.1 %copy-start = (f32[32,64,64]{2,1,0:T(8,128)S(1)}, f32[32,64,64]{2,1,0:T(8,128)}, u32[]{:S(2)}) copy-start(f32[32,64,64]{2,1,0:T(8,128)} %param.15) | copy-start | bytes 1572868
  2.6 13.0 %collective-permute-start.4 = (f32[16,64]{1,0:T(8,128)S(1)}, f32[16,64]{1,0:T(8,128)S(1)}, u32[]{:S(2)}, u32[]{:S(2)}) collective-permute-start(f32[16,64]{1,0:T(8,128)S(1)} %get-tuple-element.31), channel_id=1, source_target_pairs={{0,1},{1,2},{2,3},{3,0},{4,5},{5,6},{6,7},{7,4},{8,9},{9,10},{10,1... | collective-permute-start | bytes 12296 | tf_op jit(solution)/shard_map/ppermute | solution.py:20
  6.6 9.0 %collective-permute-start.5 = (f32[16,64]{1,0:T(8,128)S(1)}, f32[16,64]{1,0:T(8,128)S(1)}, u32[]{:S(2)}, u32[]{:S(2)}) collective-permute-start(f32[16,64]{1,0:T(8,128)S(1)} %get-tuple-element.33), channel_id=1, source_target_pairs={{0,2},{1,3},{2,0},{3,1},{4,6},{5,7},{6,4},{7,5},{8,10},{9,11},{10,... | collective-permute-start | bytes 12296 | tf_op jit(solution)/shard_map/ppermute | solution.py:20
  10.9 4.7 %collective-permute-start.6 = (f32[16,64]{1,0:T(8,128)S(1)}, f32[16,64]{1,0:T(8,128)S(1)}, u32[]{:S(2)}, u32[]{:S(2)}) collective-permute-start(f32[16,64]{1,0:T(8,128)S(1)} %get-tuple-element.32), channel_id=1, source_target_pairs={{0,3},{1,0},{2,1},{3,2},{4,7},{5,4},{6,5},{7,6},{8,11},{9,8},{10,9... | collective-permute-start | bytes 12296 | tf_op jit(solution)/shard_map/ppermute | solution.py:20
  17.5 19.6 %copy-start.9 = (f32[3,1024]{1,0:T(4,128)S(1)}, f32[3,1024]{1,0:T(4,128)}, u32[]{:S(2)}) copy-start(f32[3,1024]{1,0:T(4,128)} %param.11) | copy-start | bytes 36868
  17.5 26.6 %copy-start.5 = (f32[64,1024]{1,0:T(8,128)S(1)}, f32[64,1024]{1,0:T(8,128)}, u32[]{:S(2)}) copy-start(f32[64,1024]{1,0:T(8,128)} %param.10) | copy-start | bytes 786436
  17.5 32.5 %copy-start.31 = (s32[4,8]{1,0:T(4,128)S(1)}, s32[4,8]{1,0:T(4,128)}, u32[]{:S(2)}) copy-start(s32[4,8]{1,0:T(4,128)} %param.19) | copy-start | bytes 388
  17.5 32.6 %copy-start.32 = (s32[4,8]{1,0:T(4,128)S(1)}, s32[4,8]{1,0:T(4,128)}, u32[]{:S(2)}) copy-start(s32[4,8]{1,0:T(4,128)} %param.18) | copy-start | bytes 388
  17.5 82.0 %all-to-all-start = ((f32[128,40,128]{2,1,0:T(8,128)}), f32[128,40,128]{2,1,0:T(8,128)}, u32[]{:S(2)}, u32[]{:S(2)}) async-start(f32[128,40,128]{2,1,0:T(8,128)} %pad_maximum_fusion), calls=%async_computation | async-start | bytes 5242880 | tf_op jit(solution)/shard_map/all_to_all | solution.py:59
  37.1 15.6 %collective-permute-start = (f32[3,256]{1,0:T(4,128)S(1)}, f32[3,256]{1,0:T(4,128)S(1)}, u32[]{:S(2)}, u32[]{:S(2)}) collective-permute-start(f32[3,256]{1,0:T(4,128)S(1)} %get-tuple-element.38), channel_id=1, source_target_pairs={{0,1},{1,2},{2,3},{3,4},{4,5},{5,6},{6,7},{7,8},{8,9},{9,10},{10,1... | collective-permute-start | bytes 9224 | tf_op jit(solution)/shard_map/ppermute | solution.py:14
  39.0 13.7 %collective-permute-start.2 = (f32[3,256]{1,0:T(4,128)S(1)}, f32[3,256]{1,0:T(4,128)S(1)}, u32[]{:S(2)}, u32[]{:S(2)}) collective-permute-start(f32[3,256]{1,0:T(4,128)S(1)} %get-tuple-element.39), channel_id=1, source_target_pairs={{1,0},{2,1},{3,2},{4,3},{5,4},{6,5},{7,6},{8,7},{9,8},{10,9},{11,1... | collective-permute-start | bytes 9224 | tf_op jit(solution)/shard_map/ppermute | solution.py:15
  44.2 8.7 %collective-permute-start.3 = (f32[64,256]{1,0:T(8,128)S(1)}, f32[64,256]{1,0:T(8,128)S(1)}, u32[]{:S(2)}, u32[]{:S(2)}) collective-permute-start(f32[64,256]{1,0:T(8,128)S(1)} %get-tuple-element.19), channel_id=1, source_target_pairs={{1,0},{2,1},{3,2},{4,3},{5,4},{6,5},{7,6},{8,7},{9,8},{10,9},{11,1... | collective-permute-start | bytes 196616 | tf_op jit(solution)/shard_map/ppermute | solution.py:15
  48.1 7.2 %collective-permute-start.1 = (f32[64,256]{1,0:T(8,128)S(1)}, f32[64,256]{1,0:T(8,128)S(1)}, u32[]{:S(2)}, u32[]{:S(2)}) collective-permute-start(f32[64,256]{1,0:T(8,128)S(1)} %get-tuple-element.18), channel_id=1, source_target_pairs={{0,1},{1,2},{2,3},{3,4},{4,5},{5,6},{6,7},{7,8},{8,9},{9,10},{10,1... | collective-permute-start | bytes 196616 | tf_op jit(solution)/shard_map/ppermute | solution.py:14
  57.0 44.2 %copy-start.2 = (f32[1,128,16,64]{1,3,2,0:T(8,128)S(1)}, f32[1,128,16,64]{1,3,2,0:T(8,128)}, u32[]{:S(2)}) copy-start(f32[1,128,16,64]{1,3,2,0:T(8,128)} %param.16) | copy-start | bytes 1572868
  57.0 54.7 %copy-start.10 = (s32[1024]{0:T(1024)S(1)}, s32[1024]{0:T(1024)}, u32[]{:S(2)}) copy-start(s32[1024]{0:T(1024)} %pad_clamp_fusion.1) | copy-start | bytes 12292
  102.4 12.6 %collective-permute-start.7 = (f32[32,128]{1,0:T(8,128)S(1)}, f32[32,128]{1,0:T(8,128)}, u32[]{:S(2)}, u32[]{:S(2)}) collective-permute-start(f32[32,128]{1,0:T(8,128)S(1)} %pad_maximum_fusion.14), channel_id=1, source_target_pairs={{0,1},{1,2},{2,3},{3,0},{4,5},{5,6},{6,7},{7,4},{8,9},{9,10},{10,1... | collective-permute-start | bytes 49160 | tf_op jit(solution)/shard_map/ppermute | solution.py:20
  104.3 10.7 %collective-permute-start.8 = (f32[32,128]{1,0:T(8,128)S(1)}, f32[32,128]{1,0:T(8,128)}, u32[]{:S(2)}, u32[]{:S(2)}) collective-permute-start(f32[32,128]{1,0:T(8,128)S(1)} %pad_maximum_fusion.14), channel_id=1, source_target_pairs={{0,2},{1,3},{2,0},{3,1},{4,6},{5,7},{6,4},{7,5},{8,10},{9,11},{10,... | collective-permute-start | bytes 49160 | tf_op jit(solution)/shard_map/ppermute | solution.py:20
  109.8 5.2 %collective-permute-start.9 = (f32[32,128]{1,0:T(8,128)S(1)}, f32[32,128]{1,0:T(8,128)}, u32[]{:S(2)}, u32[]{:S(2)}) collective-permute-start(f32[32,128]{1,0:T(8,128)S(1)} %pad_maximum_fusion.14), channel_id=1, source_target_pairs={{0,3},{1,0},{2,1},{3,2},{4,7},{5,4},{6,5},{7,6},{8,11},{9,8},{10,9... | collective-permute-start | bytes 49160 | tf_op jit(solution)/shard_map/ppermute | solution.py:20
  117.9 12.0 %collective-permute-start.12 = (f32[16,64]{1,0:T(8,128)S(1)}, f32[16,64]{1,0:T(8,128)S(1)}, u32[]{:S(2)}, u32[]{:S(2)}) collective-permute-start(f32[16,64]{1,0:T(8,128)S(1)} %get-tuple-element.26), channel_id=1, source_target_pairs={{0,1},{1,2},{2,3},{3,0},{4,5},{5,6},{6,7},{7,4},{8,9},{9,10},{10,1... | collective-permute-start | bytes 12296 | tf_op jit(solution)/shard_map/ppermute | solution.py:20
  121.3 8.6 %collective-permute-start.13 = (f32[16,64]{1,0:T(8,128)S(1)}, f32[16,64]{1,0:T(8,128)S(1)}, u32[]{:S(2)}, u32[]{:S(2)}) collective-permute-start(f32[16,64]{1,0:T(8,128)S(1)} %get-tuple-element.28), channel_id=1, source_target_pairs={{0,2},{1,3},{2,0},{3,1},{4,6},{5,7},{6,4},{7,5},{8,10},{9,11},{10,... | collective-permute-start | bytes 12296 | tf_op jit(solution)/shard_map/ppermute | solution.py:20
  123.5 6.4 %collective-permute-start.14 = (f32[16,64]{1,0:T(8,128)S(1)}, f32[16,64]{1,0:T(8,128)S(1)}, u32[]{:S(2)}, u32[]{:S(2)}) collective-permute-start(f32[16,64]{1,0:T(8,128)S(1)} %get-tuple-element.27), channel_id=1, source_target_pairs={{0,3},{1,0},{2,1},{3,2},{4,7},{5,4},{6,5},{7,6},{8,11},{9,8},{10,9... | collective-permute-start | bytes 12296 | tf_op jit(solution)/shard_map/ppermute | solution.py:20
  133.3 14.4 %copy-start.4 = (f32[64,4,256]{2,0,1:T(8,128)S(1)}, f32[64,4,256]{2,0,1:T(8,128)}, u32[]{:S(2)}) copy-start(f32[64,4,256]{2,0,1:T(8,128)} %copy-done.3) | copy-start | bytes 786436
  133.3 19.7 %copy-start.14 = (f32[4,256]{1,0:T(4,128)S(1)}, f32[4,256]{1,0:T(4,128)}, u32[]{:S(2)}) copy-start(f32[4,256]{1,0:T(4,128)} %copy-done.13) | copy-start | bytes 12292
  133.3 19.7 %copy-start.16 = (f32[4,256]{1,0:T(4,128)S(1)}, f32[4,256]{1,0:T(4,128)}, u32[]{:S(2)}) copy-start(f32[4,256]{1,0:T(4,128)} %copy-done.15) | copy-start | bytes 12292
  133.3 19.7 %copy-start.18 = (f32[4,256]{1,0:T(4,128)S(1)}, f32[4,256]{1,0:T(4,128)}, u32[]{:S(2)}) copy-start(f32[4,256]{1,0:T(4,128)} %copy-done.17) | copy-start | bytes 12292
  133.3 76.9 %all-to-all-start.1 = ((f32[128,40,128]{2,1,0:T(8,128)}), f32[128,40,128]{2,1,0:T(8,128)}, u32[]{:S(2)}, u32[]{:S(2)}) async-start(f32[128,40,128]{2,1,0:T(8,128)} %pad_maximum_fusion.1), calls=%async_computation.1 | async-start | bytes 5242880 | tf_op jit(solution)/shard_map/all_to_all | solution.py:59
  147.8 8.2 %collective-permute-start.11 = (f32[64,256]{1,0:T(8,128)S(1)}, f32[64,256]{1,0:T(8,128)S(1)}, u32[]{:S(2)}, u32[]{:S(2)}) collective-permute-start(f32[64,256]{1,0:T(8,128)S(1)} %get-tuple-element.17), channel_id=1, source_target_pairs={{1,0},{2,1},{3,2},{4,3},{5,4},{6,5},{7,6},{8,7},{9,8},{10,9},{11,1... | collective-permute-start | bytes 196616 | tf_op jit(solution)/shard_map/ppermute | solution.py:15
  154.1 7.2 %collective-permute-start.10 = (f32[64,256]{1,0:T(8,128)S(1)}, f32[64,256]{1,0:T(8,128)S(1)}, u32[]{:S(2)}, u32[]{:S(2)}) collective-permute-start(f32[64,256]{1,0:T(8,128)S(1)} %get-tuple-element.16), channel_id=1, source_target_pairs={{0,1},{1,2},{2,3},{3,4},{4,5},{5,6},{6,7},{7,8},{8,9},{9,10},{10,1... | collective-permute-start | bytes 196616 | tf_op jit(solution)/shard_map/ppermute | solution.py:14
  162.2 60.1 %copy-start.11 = (s32[1024]{0:T(1024)S(1)}, s32[1024]{0:T(1024)}, u32[]{:S(2)}) copy-start(s32[1024]{0:T(1024)} %pad_clamp_fusion.1) | copy-start | bytes 12292
  213.1 12.5 %collective-permute-start.15 = (f32[32,128]{1,0:T(8,128)S(1)}, f32[32,128]{1,0:T(8,128)S(1)}, u32[]{:S(2)}, u32[]{:S(2)}) collective-permute-start(f32[32,128]{1,0:T(8,128)S(1)} %pad_maximum_fusion.15), channel_id=1, source_target_pairs={{0,1},{1,2},{2,3},{3,0},{4,5},{5,6},{6,7},{7,4},{8,9},{9,10},{10,1... | collective-permute-start | bytes 49160 | tf_op jit(solution)/shard_map/ppermute | solution.py:20
  215.2 10.5 %collective-permute-start.16 = (f32[32,128]{1,0:T(8,128)S(1)}, f32[32,128]{1,0:T(8,128)S(1)}, u32[]{:S(2)}, u32[]{:S(2)}) collective-permute-start(f32[32,128]{1,0:T(8,128)S(1)} %pad_maximum_fusion.15), channel_id=1, source_target_pairs={{0,2},{1,3},{2,0},{3,1},{4,6},{5,7},{6,4},{7,5},{8,10},{9,11},{10,... | collective-permute-start | bytes 49160 | tf_op jit(solution)/shard_map/ppermute | solution.py:20
  220.4 5.2 %collective-permute-start.17 = (f32[32,128]{1,0:T(8,128)S(1)}, f32[32,128]{1,0:T(8,128)S(1)}, u32[]{:S(2)}, u32[]{:S(2)}) collective-permute-start(f32[32,128]{1,0:T(8,128)S(1)} %pad_maximum_fusion.15), channel_id=1, source_target_pairs={{0,3},{1,0},{2,1},{3,2},{4,7},{5,4},{6,5},{7,6},{8,11},{9,8},{10,9... | collective-permute-start | bytes 49160 | tf_op jit(solution)/shard_map/ppermute | solution.py:20
  (21 other events, 130.2 us)

commit v2 on v1

v2 whole, which is shorter than its diff:
```python
import functools
import math

import jax
import jax.numpy as jnp
from jax import lax
from jax.experimental import pallas as pl
from jax.experimental.pallas import tpu as pltpu
from jax.sharding import PartitionSpec as P

precise = lax.Precision.HIGH
MESH = pl.DeviceIdType.MESH
SIDE = 8
CORES = 2


def halo(block, axes, count):
    forward = [(i, i + 1) for i in range(count - 1)]
    backward = [(target, source) for source, target in forward]
    low = lax.ppermute(block[:, -1], axes, forward)
    high = lax.ppermute(block[:, 0], axes, backward)
    return jnp.concatenate([low[:, None], block, high[:, None]], axis=1)


def kernel_blocks(sources, targets, leaf_size):
    dist = 0.0
    for component in range(3):
        gap = sources[component][:, :, None] - targets[component][:, None, :]
        dist = dist + gap * gap
    return jnp.exp(-0.5 * dist) * (1.0 / math.sqrt(leaf_size))


def fold(values):
    half = values.shape[-2] // 2
    return jnp.concatenate([values[..., :half, :], values[..., half:, :]], axis=-1)


def unfold(values):
    half = values.shape[-1] // 2
    return jnp.concatenate([values[..., :half], values[..., half:]], axis=-2)


def ring_events():
    events = []
    reach = SIDE // 2
    for a in range(-reach, reach):
        plus, minus = (reach, reach - 1) if a % 2 == 0 else (reach - 1, reach)
        for b in range(-plus, minus + 1):
            events.append((abs(a) + abs(b), abs(b), a, b, plus, minus))
    return sorted(events)


def place():
    leaf = lax.axis_index("leaf")
    return leaf // (SIDE * CORES), (leaf // CORES) % SIDE, leaf % CORES, lax.axis_index("sub")


def leaf_of(y, z, core):
    return (y * SIDE + z) * CORES + core


def wrapped(index, step, size):
    return lax.rem(index + (step + size), size)


def exchange_kernel(
    subs,
    leaf_total,
    skeleton_ref,
    row_ref,
    parts_ref,
    edges_ref,
    gather_ref,
    halo_ref,
    sums_ref,
    ring_send,
    ring_recv,
    pair_send,
    pair_recv,
    small_send,
    small_recv,
):
    y, z, core, sub = place()
    leaf = lax.axis_index("leaf")
    rank = skeleton_ref.shape[1]
    partner = (leaf_of(y, z, 1 - core), sub)
    y_up = (leaf_of(wrapped(y, 1, SIDE), z, core), sub)
    y_down = (leaf_of(wrapped(y, -1, SIDE), z, core), sub)
    z_up = (leaf_of(y, wrapped(z, 1, SIDE), core), sub)
    z_down = (leaf_of(y, wrapped(z, -1, SIDE), core), sub)
    peers = [(leaf, wrapped(sub, step, subs)) for step in range(1, subs)]
    position = leaf * subs + sub
    total = leaf_total * subs
    after = wrapped(position, 1, total)
    before = wrapped(position, -1, total)
    after = (after // subs, after % subs)
    before = (before // subs, before % subs)

    barrier = pltpu.get_barrier_semaphore()
    others = [partner, y_up, y_down, z_up, z_down] + peers + [after, before]
    for other in others:
        pl.semaphore_signal(barrier, inc=1, device_id=other, device_id_type=MESH)

    gather_ref[0, y, z, core, :rank] = skeleton_ref[0]
    gather_ref[1, y, z, core, :rank] = skeleton_ref[1]
    gather_ref[1, y, z, core, rank:] = row_ref[...]
    pl.semaphore_wait(barrier, len(others))

    small = []
    for step, peer in enumerate(peers):
        small.append(
            pltpu.make_async_remote_copy(
                src_ref=parts_ref.at[peer[1]],
                dst_ref=sums_ref.at[step],
                send_sem=small_send.at[step],
                recv_sem=small_recv.at[step],
                device_id=peer,
                device_id_type=MESH,
            )
        )
    for way, other in enumerate((before, after)):
        small.append(
            pltpu.make_async_remote_copy(
                src_ref=edges_ref.at[way],
                dst_ref=halo_ref.at[1 - way],
                send_sem=small_send.at[subs - 1 + way],
                recv_sem=small_recv.at[subs - 1 + way],
                device_id=other,
                device_id_type=MESH,
            )
        )
    for copy in small:
        copy.start()

    def block(half, a, b):
        if half == 0:
            return gather_ref.at[0, wrapped(y, b, SIDE), wrapped(z, a, SIDE), core]
        return gather_ref.at[1, wrapped(y, a, SIDE), wrapped(z, b, SIDE), core]

    first = ((z_up, z_down), (y_up, y_down))
    second = ((y_up, y_down), (z_up, z_down))

    def ring_copy(half, a, b, landed_a, landed_b, other):
        i, j = landed_a % SIDE, landed_b % SIDE
        here = block(half, a, b)
        return pltpu.make_async_remote_copy(
            src_ref=here,
            dst_ref=here,
            send_sem=ring_send.at[half, i, j],
            recv_sem=ring_recv.at[half, i, j],
            device_id=other,
            device_id_type=MESH,
        )

    def pair_copy(half, a, b):
        here = block(half, a, b)
        return pltpu.make_async_remote_copy(
            src_ref=here,
            dst_ref=here,
            send_sem=pair_send.at[half, a % SIDE, b % SIDE],
            recv_sem=pair_recv.at[half, a % SIDE, b % SIDE],
            device_id=partner,
            device_id_type=MESH,
        )

    sent = []

    def pass_on(half, a, b, plus, minus):
        copies = []
        up, down = first[half]
        reach = SIDE // 2
        if b == 0:
            if -reach < a <= 0:
                copies.append(ring_copy(half, a, b, a - 1, b, up))
            if 0 <= a < reach - 1:
                copies.append(ring_copy(half, a, b, a + 1, b, down))
        up, down = second[half]
        if -plus < b <= 0:
            copies.append(ring_copy(half, a, b, a, b - 1, up))
        if 0 <= b < minus:
            copies.append(ring_copy(half, a, b, a, b + 1, down))
        copies.append(pair_copy(half, a, b))
        for copy in copies:
            copy.start()
        sent.extend(copies)

    events = ring_events()
    _, _, a, b, plus, minus = events[0]
    pass_on(1, a, b, plus, minus)
    for copy in small[: subs - 1]:
        copy.wait_recv()
    parent = parts_ref[sub]
    for step in range(subs - 1):
        parent = parent + sums_ref[step]
    gather_ref[0, y, z, core, rank:] = parent
    pass_on(0, a, b, plus, minus)
    for _, _, a, b, plus, minus in events[1:]:
        for half in (1, 0):
            ring_copy(half, a, b, a, b, partner).wait_recv()
            pass_on(half, a, b, plus, minus)
    for copy in small:
        copy.wait_send()
    for copy in small[subs - 1 :]:
        copy.wait_recv()
    for copy in sent:
        copy.wait_send()
    for _, _, a, b, _, _ in events:
        for half in (0, 1):
            pair_copy(half, a, b).wait_recv()


def exchange(skeleton, row, parts, edges, subs, leaf_total):
    rows = skeleton.shape[1] + row.shape[0]
    lanes = skeleton.shape[2]
    vmem = pl.BlockSpec(memory_space=pltpu.VMEM)
    dma = pltpu.SemaphoreType.DMA
    return pl.pallas_call(
        functools.partial(exchange_kernel, subs, leaf_total),
        out_shape=(
            jax.ShapeDtypeStruct((2, SIDE, SIDE, CORES, rows, lanes), jnp.float32),
            jax.ShapeDtypeStruct(edges.shape, jnp.float32),
        ),
        in_specs=[vmem] * 4,
        out_specs=(vmem, vmem),
        scratch_shapes=[
            pltpu.VMEM((subs - 1,) + parts.shape[1:], jnp.float32),
            dma((2, SIDE, SIDE)),
            dma((2, SIDE, SIDE)),
            dma((2, SIDE, SIDE)),
            dma((2, SIDE, SIDE)),
            dma((subs + 1,)),
            dma((subs + 1,)),
        ],
        compiler_params=pltpu.CompilerParams(collective_id=0, has_side_effects=True),
        name="exchange",
    )(skeleton, row, parts, edges)


def sum_kernel(subs, in_ref, out_ref, sums_ref, send_sem, recv_sem):
    leaf, sub = lax.axis_index("leaf"), lax.axis_index("sub")
    peers = [(leaf, wrapped(sub, step, subs)) for step in range(1, subs)]
    barrier = pltpu.get_barrier_semaphore()
    for peer in peers:
        pl.semaphore_signal(barrier, inc=1, device_id=peer, device_id_type=MESH)
    pl.semaphore_wait(barrier, subs - 1)
    copies = [
        pltpu.make_async_remote_copy(
            src_ref=in_ref,
            dst_ref=sums_ref.at[step],
            send_sem=send_sem.at[step],
            recv_sem=recv_sem.at[step],
            device_id=peer,
            device_id_type=MESH,
        )
        for step, peer in enumerate(peers)
    ]
    for copy in copies:
        copy.start()
    result = in_ref[...]
    for step, copy in enumerate(copies):
        copy.wait_recv()
        result = result + sums_ref[step]
    out_ref[...] = result
    for copy in copies:
        copy.wait_send()


def sum_over_sub(values, subs):
    vmem = pl.BlockSpec(memory_space=pltpu.VMEM)
    dma = pltpu.SemaphoreType.DMA
    return pl.pallas_call(
        functools.partial(sum_kernel, subs),
        out_shape=jax.ShapeDtypeStruct(values.shape, jnp.float32),
        in_specs=[vmem],
        out_specs=vmem,
        scratch_shapes=[
            pltpu.VMEM((subs - 1,) + values.shape, jnp.float32),
            dma((subs - 1,)),
            dma((subs - 1,)),
        ],
        compiler_params=pltpu.CompilerParams(collective_id=1, has_side_effects=True),
        name="sum_over_sub",
    )(values)


def one_product(field, near_kernels, basis, up, down, couplings, top, row, slots, blocks):
    rhs, leaves, size = field.shape
    rank = basis.shape[1]
    subs = lax.axis_size("sub")
    leaf_total = lax.axis_size("leaf")
    leaf = lax.axis_index("leaf")
    skeleton = jnp.einsum("pla,lra->lpr", field, basis, precision=precise)
    parent_t = jnp.einsum("lpr,lrq->qp", skeleton, up, precision=precise)
    parts = fold(parent_t.reshape(subs, rank // subs, rhs))
    pairs = jnp.concatenate([skeleton[0::2], skeleton[1::2]], axis=-1)
    edges = jnp.stack([field[:, 0], field[:, -1]])
    gathered, sides = exchange(pairs, row, parts, edges, subs, leaf_total)
    gathered = gathered.reshape(2, leaf_total, -1, 2 * rank)
    parents = unfold(gathered[0, :, rhs:])
    top_part = jnp.einsum("erp,erq->pq", parents, top, precision=precise)
    top_term = unfold(sum_over_sub(fold(top_part), subs))
    padded = jnp.concatenate([sides[0][:, None], field, sides[1][:, None]], axis=1)
    near = 0.0
    for side in range(3):
        near = near + jnp.einsum(
            "plb,lba->pla", padded[:, side : side + leaves], near_kernels[side], precision=precise
        )
    chosen = lax.dynamic_index_in_dim(gathered[1, :, rhs], leaf, 1, keepdims=False)[slots]
    chosen = chosen.astype(jnp.int32)
    both = gathered[chosen // 2, slots, :rhs]
    source = jnp.where((chosen % 2 == 0)[..., None, None], both[..., :rank], both[..., rank:])
    far = jnp.einsum("lkpr,lkrq->lpq", source, couplings[blocks], precision=precise)
    coef = far + jnp.einsum("pr,lrq->lpq", top_term, down, precision=precise)
    return near + jnp.einsum("lpr,lra->pla", coef, basis, precision=precise)


def local(
    field, coords, basis, up_transfer, down_transfer, couplings, top_coupling, send_leaf, list_slot, list_block
):
    rhs = field.shape[0]
    leaves, _, size = basis.shape
    subs = lax.axis_size("sub")
    count = lax.axis_size("leaf") * subs
    position = lax.axis_index("leaf") * subs + lax.axis_index("sub")
    points = coords.reshape(3, leaves, size)
    all_points = halo(points, ("leaf", "sub"), count)
    near_kernels = []
    for side in range(3):
        index = position * leaves + jnp.arange(leaves) + (side - 1)
        present = (index >= 0) & (index < count * leaves)
        values = kernel_blocks(all_points[:, side : side + leaves], points, size)
        near_kernels.append(jnp.where(present[:, None, None], values, 0.0))
    row = jnp.broadcast_to(send_leaf.reshape(1, -1).astype(jnp.float32), (8, send_leaf.size))
    current = field.reshape(rhs, leaves, size)
    for repeat in range(2):
        current = one_product(
            current,
            near_kernels,
            basis,
            up_transfer,
            down_transfer,
            couplings,
            top_coupling[0],
            row,
            list_slot,
            list_block,
        )
    return current.reshape(rhs, leaves * size)


def solution(mesh):
    joined = ("leaf", "sub")
    in_specs = (
        P(None, joined),
        P(None, joined),
        P(joined, None, None),
        P(joined, None, None),
        P(joined, None, None),
        P(joined, None, None),
        P("leaf", None, "sub", None),
        P("leaf", "sub", None, None),
        P(joined, None),
        P(joined, None),
    )
    return jax.shard_map(local, mesh=mesh, in_specs=in_specs, out_specs=P(None, joined), check_vma=False)
```

time: 228 us -> 208 us (0.912)
  Pallas kernels: 0 us -> 122 us
  waiting for transfers between devices: 96.4 us -> 0.01 us
  starting transfers between devices: 93.3 us -> 7.69 us
  local copies, waits for them, and re-layouts: 13.6 us -> 47.9 us
  matrix products: 14.9 us -> 18.7 us
  other arithmetic: 7.66 us -> 9.96 us
    pallas_call x0 -> x4, Pallas kernels: none -> 122 us  [the longest x2 109 us: exchange(): pl.pallas_call(functools.partial(exchange_kernel, subs, leaf_total), out_...]
    all_to_all x2 -> x0, waiting for transfers between devices: 90.5 us -> none  [one_product(): lax.all_to_all(outgoing, 'leaf', split_axis=0, concat_axis=0, tiled=True)]
    ppermute x12 -> x0, starting transfers between devices: 39.5 us -> none  [shifted(): lax.ppermute(values, axis, [(i, (i + step) % count) for i in range(count)])]
    all_to_all x2 -> x0, starting transfers between devices: 34 us -> none  [one_product(): lax.all_to_all(outgoing, 'leaf', split_axis=0, concat_axis=0, tiled=True)]
    reshape x0 -> x2, local copies, waits for them, and re-layouts: none -> 18.4 us  [one_product(): gathered = gathered.reshape(2, leaf_total, -1, 2 * rank)]
    ppermute x3 -> x1, starting transfers between devices: 14.2 us -> 3.75 us  [halo(): high = lax.ppermute(block[:, 0], axes, backward)]
    ppermute x3 -> x1, waiting for transfers between devices: 5.85 us -> 0.01 us  [halo(): low = lax.ppermute(block[:, -1], axes, forward)]
    slice x0 -> x6, local copies, waits for them, and re-layouts: none -> 4.33 us  [the longest x2 2.15 us: one_product(): parents = unfold(gathered[0, :, rhs:])]
  transfers between devices with their start and end apart: 20 -> 2, of which waited for: 4 -> 0; matrix products, arithmetic and copies ran while one was open for 8% -> 16% of each run, Pallas kernels for 0% -> 32%
where the time goes in v2:
time: 208 us; the launch traced here: 207 us
  Pallas kernels  122 us (59%)
  local copies, waits for them, and re-layouts  47.9 us (23%)
  matrix products  18.7 us (9%)
  other arithmetic  9.96 us (5%)
  starting transfers between devices  7.69 us (4%)
    pallas_call x2, Pallas kernels, exchange(): pl.pallas_call(functools.partial(exchange_kernel, subs, leaf_total), out_...  109 us
    reshape x2, local copies, waits for them, and re-layouts, one_product(): gathered = gathered.reshape(2, leaf_total, -1, 2 * rank)  18.4 us
    pallas_call x2, Pallas kernels, sum_over_sub(): pl.pallas_call(functools.partial(sum_kernel, subs), out_shape=jax.ShapeDt...  12.7 us
    dot_general x6, matrix products, one_product(): jnp.einsum('plb,lba->pla', padded[:, side:side + leaves], near_kernels[si...  10.6 us
    gather x2, local copies, waits for them, and re-layouts, one_product(): both = gathered[chosen // 2, slots, :rhs]  6.16 us
  transfers between devices with their start and end apart: 2, of which 0 were waited for; matrix products, arithmetic and copies ran while one was open for 16% of the time, Pallas kernels for 32%

profile of v2, /device:TPU:1, one launch (start us, length us, event | category | flops | bytes accessed | tf_op | source)
XLA Modules:
  0.0 206.7 jit_solution(10463429731475278082)
XLA Ops:
  0.0 1.4 slice_bitcast_fusion.8
  1.4 3.9 %collective-permute-start = (f32[3,256]{1,0:T(4,128)}, f32[3,256]{1,0:T(4,128)}, u32[]{:S(2)}, u32[]{:S(2)}) collective-permute-start(f32[3,256]{1,0:T(4,128)} %get-tuple-element.45), channel_id=1, source_target_pairs={{0,1},{1,2},{2,3},{3,4},{4,5},{5,6},{6,7},{7,8},{8,9},{9,10},{10,1... | collective-permute-start | bytes 9224 | tf_op jit(solution)/shard_map/ppermute | solution.py:20
  5.3 3.7 %collective-permute-start.1 = (f32[3,256]{1,0:T(4,128)}, f32[3,256]{1,0:T(4,128)}, u32[]{:S(2)}, u32[]{:S(2)}) collective-permute-start(f32[3,256]{1,0:T(4,128)} %get-tuple-element.44), channel_id=1, source_target_pairs={{1,0},{2,1},{3,2},{4,3},{5,4},{6,5},{7,6},{8,7},{9,8},{10,9},{11,1... | collective-permute-start | bytes 9224 | tf_op jit(solution)/shard_map/ppermute | solution.py:21
  9.1 1.0 copy.57
  10.8 1.3 fusion.129
  12.1 1.1 convolution_bitcast_fusion.9
  16.7 58.8 %exchange.2 = (f32[2,8,8,2,72,128]{5,4,3,2,1,0:T(8,128)}, f32[2,64,256]{2,1,0:T(8,128)}) custom-call(f32[2,64,128]{2,1,0:T(8,128)} %pad_maximum_fusion.10.skeleton_ref, f32[8,128]{1,0:T(8,128)} %broadcast_in_dim.68.row_ref, f32[4,8,128]{2,1,0:T(8,128)} %pad_maximum_fusion.12.parts_ref, f32[2,64,256]{2,1,0:T(8,128)} %pad_maximum_fusion.8.edges_ref), custom_call_target="tpu_custom_call" | custom-call | tf_op jit(solution)/shard_map/exchange/pallas_call | solution.py:217
  75.5 1.1 slice.251
  76.6 1.1 slice.248
  77.7 9.2 %copy.31 = f32[2,128,72,128]{3,1,0,2:T(8,128)} copy(f32[2,128,72,128]{3,2,1,0:T(8,128)} %bitcast.134) | data formatting | bytes 18874368 | tf_op jit(solution)/shard_map/reshape | solution.py:298
  90.2 6.3 %sum_over_sub.2 = f32[32,128]{1,0:T(8,128)} custom-call(f32[32,128]{1,0:T(8,128)} %pad_maximum_fusion.13.in_ref), custom_call_target="tpu_custom_call" | custom-call | tf_op jit(solution)/shard_map/sum_over_sub/pallas_call | solution.py:271
  96.6 1.5 fusion.139
  100.1 3.1 %gather_fusion.1 = f32[32,64,128]{2,0,1:T(8,128)S(1)} fusion(f32[2,128,72,128]{3,1,0,2:T(8,128)} %copy.31, s32[32]{0:T(128)S(1)} %reshape.243), kind=kCustom, calls=%fused_computation.1 | custom fusion | bytes 2097536 | tf_op jit(solution)/shard_map/gather | solution.py:310
  104.5 1.3 convolution_bitcast_fusion.5
  105.7 1.1 fusion.6
  109.8 1.9 fusion.10
  111.7 1.9 convolution_add_fusion.3
  113.7 2.1 %fusion.4 = f32[64,4,256]{2,0,1:T(8,128)S(1)} fusion(f32[4,256,64]{1,2,0:T(8,128)S(1)} %convolution_add_fusion.3, f32[4,256]{1,0:T(4,128)S(1)} %get-tuple-element.48, f32[4,256]{1,0:T(4,128)S(1)} %get-tuple-element.47, f32[4,256]{1,0:T(4,128)S(1)} %get-tuple-element.46, f32[4,256]{1,0:T(4,128)S(1)} %sub.145, f32[4,256]{1,0:T(4,128)S(1)} %sub.140, ...), kind=kOutput, calls=%fused_computation.14 | convolution fusion | flops 103677952 | bytes 876548 | tf_op jit(solution)/shard_map/plb,lba->pla/dot_general | solution.py:305
  118.8 50.3 %exchange.3 = (f32[2,8,8,2,72,128]{5,4,3,2,1,0:T(8,128)}, f32[2,64,256]{2,1,0:T(8,128)}) custom-call(f32[2,64,128]{2,1,0:T(8,128)} %pad_maximum_fusion.11.skeleton_ref, f32[8,128]{1,0:T(8,128)} %broadcast_in_dim.68.row_ref, f32[4,8,128]{2,1,0:T(8,128)} %pad_maximum_fusion.14.parts_ref, f32[2,64,256]{2,1,0:T(8,128)} %pad_maximum_fusion.9.edges_ref), custom_call_target="tpu_custom_call" | custom-call | tf_op jit(solution)/shard_map/exchange/pallas_call | solution.py:217
  169.1 1.1 slice.263
  170.2 9.2 %copy.35 = f32[2,128,72,128]{3,1,0,2:T(8,128)} copy(f32[2,128,72,128]{3,2,1,0:T(8,128)} %bitcast.136) | data formatting | bytes 18874368 | tf_op jit(solution)/shard_map/reshape | solution.py:298
  179.4 1.1 slice.260
  183.4 1.1 copy.47
  184.5 1.1 fusion.130
  186.7 6.3 %sum_over_sub.3 = f32[32,128]{1,0:T(8,128)} custom-call(f32[32,128]{1,0:T(8,128)} %pad_maximum_fusion.15.in_ref), custom_call_target="tpu_custom_call" | custom-call | tf_op jit(solution)/shard_map/sum_over_sub/pallas_call | solution.py:271
  193.0 1.5 fusion.138
  195.1 3.1 %gather_fusion.4 = f32[32,64,128]{2,0,1:T(8,128)S(1)} fusion(f32[2,128,72,128]{3,1,0,2:T(8,128)} %copy.35, s32[32]{0:T(128)S(1)} %reshape.265), kind=kCustom, calls=%fused_computation.4 | custom fusion | bytes 2097536 | tf_op jit(solution)/shard_map/gather | solution.py:310
  198.3 1.1 slice_select_fusion
  199.4 1.3 convolution_bitcast_fusion.4
  200.7 1.9 fusion.9
  202.6 1.9 convolution_add_fusion.1
  204.6 0.9 fusion.3
  (140 shorter events, 22.4 us)
Async XLA Ops:
  0.0 103.6 %copy-start = (f32[32,64,64]{2,1,0:T(8,128)S(1)}, f32[32,64,64]{2,1,0:T(8,128)}, u32[]{:S(2)}) copy-start(f32[32,64,64]{2,1,0:T(8,128)} %param.15) | copy-start | bytes 1572868
  1.4 106.9 %collective-permute-start = (f32[3,256]{1,0:T(4,128)}, f32[3,256]{1,0:T(4,128)}, u32[]{:S(2)}, u32[]{:S(2)}) collective-permute-start(f32[3,256]{1,0:T(4,128)} %get-tuple-element.45), channel_id=1, source_target_pairs={{0,1},{1,2},{2,3},{3,4},{4,5},{5,6},{6,7},{7,8},{8,9},{9,10},{10,1... | collective-permute-start | bytes 9224 | tf_op jit(solution)/shard_map/ppermute | solution.py:20
  5.3 103.7 %collective-permute-start.1 = (f32[3,256]{1,0:T(4,128)}, f32[3,256]{1,0:T(4,128)}, u32[]{:S(2)}, u32[]{:S(2)}) collective-permute-start(f32[3,256]{1,0:T(4,128)} %get-tuple-element.44), channel_id=1, source_target_pairs={{1,0},{2,1},{3,2},{4,3},{5,4},{6,5},{7,6},{8,7},{9,8},{10,9},{11,1... | collective-permute-start | bytes 9224 | tf_op jit(solution)/shard_map/ppermute | solution.py:21
  77.7 9.5 %copy-start.14 = (s32[4,8]{1,0:T(4,128)S(1)}, s32[4,8]{1,0:T(4,128)}, u32[]{:S(2)}) copy-start(s32[4,8]{1,0:T(4,128)} %param.18) | copy-start | bytes 388
  77.7 10.5 %copy-start.11 = (f32[3,1024]{1,0:T(4,128)S(1)}, f32[3,1024]{1,0:T(4,128)}, u32[]{:S(2)}) copy-start(f32[3,1024]{1,0:T(4,128)} %param.11) | copy-start | bytes 36868
  77.7 11.4 %copy-start.2 = (f32[1,128,16,64]{1,3,2,0:T(8,128)S(1)}, f32[1,128,16,64]{1,3,2,0:T(8,128)}, u32[]{:S(2)}) copy-start(f32[1,128,16,64]{1,3,2,0:T(8,128)} %param.16) | copy-start | bytes 1572868
  77.7 20.4 %copy-start.32 = (s32[4,8]{1,0:T(4,128)S(1)}, s32[4,8]{1,0:T(4,128)}, u32[]{:S(2)}) copy-start(s32[4,8]{1,0:T(4,128)} %param.19) | copy-start | bytes 388
  77.7 21.1 %copy-start.9 = (f32[2,64,256]{2,1,0:T(8,128)S(1)}, f32[2,64,256]{2,1,0:T(8,128)}, u32[]{:S(2)}) copy-start(f32[2,64,256]{2,1,0:T(8,128)} %get-tuple-element.9) | copy-start | bytes 393220
  103.2 12.6 %copy-start.1 = (f32[4,64,256]{2,1,0:T(8,128)S(1)}, f32[4,64,256]{2,1,0:T(8,128)}, u32[]{:S(2)}) copy-start(f32[4,64,256]{2,1,0:T(8,128)} %param.12) | copy-start | bytes 786436
  103.6 12.8 %copy-start.7 = (f32[4,64,64]{2,1,0:T(8,128)S(1)}, f32[4,64,64]{2,1,0:T(8,128)}, u32[]{:S(2)}) copy-start(f32[4,64,64]{2,1,0:T(8,128)} %param.13) | copy-start | bytes 196612
  106.9 6.7 %copy-start.34 = (pred[4]{0:T(512)(128)(4,1)}, pred[4]{0:T(512)(128)(4,1)S(1)}, u32[]{:S(2)}) copy-start(pred[4]{0:T(512)(128)(4,1)S(1)} %compare_and_fusion.1) | copy-start | bytes 16
  108.3 71.1 %copy-start.17 = (f32[4,256]{1,0:T(4,128)}, f32[4,256]{1,0:T(4,128)S(1)}, u32[]{:S(2)}) copy-start(f32[4,256]{1,0:T(4,128)S(1)} %sub.135) | copy-start | bytes 12292
  108.3 5.3 %copy-start.19 = (f32[4,256]{1,0:T(4,128)}, f32[4,256]{1,0:T(4,128)S(1)}, u32[]{:S(2)}) copy-start(f32[4,256]{1,0:T(4,128)S(1)} %sub.140) | copy-start | bytes 12292
  108.3 5.3 %copy-start.21 = (f32[4,256]{1,0:T(4,128)}, f32[4,256]{1,0:T(4,128)S(1)}, u32[]{:S(2)}) copy-start(f32[4,256]{1,0:T(4,128)S(1)} %sub.145) | copy-start | bytes 12292
  109.7 3.9 %copy-start.23 = (f32[4,256]{1,0:T(4,128)}, f32[4,256]{1,0:T(4,128)S(1)}, u32[]{:S(2)}) copy-start(f32[4,256]{1,0:T(4,128)S(1)} %get-tuple-element.46) | copy-start | bytes 12292
  109.7 3.9 %copy-start.25 = (f32[4,256]{1,0:T(4,128)}, f32[4,256]{1,0:T(4,128)S(1)}, u32[]{:S(2)}) copy-start(f32[4,256]{1,0:T(4,128)S(1)} %get-tuple-element.47) | copy-start | bytes 12292
  109.8 3.9 %copy-start.27 = (f32[4,256]{1,0:T(4,128)}, f32[4,256]{1,0:T(4,128)S(1)}, u32[]{:S(2)}) copy-start(f32[4,256]{1,0:T(4,128)S(1)} %get-tuple-element.48) | copy-start | bytes 12292
  116.0 53.0 %copy-start.4 = (f32[64,4,256]{2,0,1:T(8,128)}, f32[64,4,256]{2,0,1:T(8,128)S(1)}, u32[]{:S(2)}) copy-start(f32[64,4,256]{2,0,1:T(8,128)S(1)} %fusion.2) | copy-start | bytes 786436
  170.1 10.6 %copy-start.16 = (s32[1024]{0:T(1024)S(1)}, s32[1024]{0:T(1024)}, u32[]{:S(2)}) copy-start(s32[1024]{0:T(1024)} %copy-done.15) | copy-start | bytes 12292
  170.2 15.4 %copy-start.3 = (f32[1,128,16,64]{1,3,2,0:T(8,128)S(1)}, f32[1,128,16,64]{1,3,2,0:T(8,128)}, u32[]{:S(2)}) copy-start(f32[1,128,16,64]{1,3,2,0:T(8,128)} %param.16) | copy-start | bytes 1572868
  181.5 19.2 %copy-start.10 = (f32[2,64,256]{2,1,0:T(8,128)S(1)}, f32[2,64,256]{2,1,0:T(8,128)}, u32[]{:S(2)}) copy-start(f32[2,64,256]{2,1,0:T(8,128)} %get-tuple-element.11) | copy-start | bytes 393220
  181.5 19.2 %copy-start.18 = (f32[4,256]{1,0:T(4,128)S(1)}, f32[4,256]{1,0:T(4,128)}, u32[]{:S(2)}) copy-start(f32[4,256]{1,0:T(4,128)} %copy-done.17) | copy-start | bytes 12292
  194.5 8.1 %copy-start.20 = (f32[4,256]{1,0:T(4,128)S(1)}, f32[4,256]{1,0:T(4,128)}, u32[]{:S(2)}) copy-start(f32[4,256]{1,0:T(4,128)} %copy-done.19) | copy-start | bytes 12292
  195.1 9.4 %copy-start.22 = (f32[4,256]{1,0:T(4,128)S(1)}, f32[4,256]{1,0:T(4,128)}, u32[]{:S(2)}) copy-start(f32[4,256]{1,0:T(4,128)} %copy-done.21) | copy-start | bytes 12292
  198.2 6.3 %copy-start.5 = (f32[64,4,256]{2,0,1:T(8,128)S(1)}, f32[64,4,256]{2,0,1:T(8,128)}, u32[]{:S(2)}) copy-start(f32[64,4,256]{2,0,1:T(8,128)} %copy-done.4) | copy-start | bytes 786436
  198.2 6.3 %copy-start.24 = (f32[4,256]{1,0:T(4,128)S(1)}, f32[4,256]{1,0:T(4,128)}, u32[]{:S(2)}) copy-start(f32[4,256]{1,0:T(4,128)} %copy-done.23) | copy-start | bytes 12292
  198.3 6.3 %copy-start.26 = (f32[4,256]{1,0:T(4,128)S(1)}, f32[4,256]{1,0:T(4,128)}, u32[]{:S(2)}) copy-start(f32[4,256]{1,0:T(4,128)} %copy-done.25) | copy-start | bytes 12292
  198.3 6.3 %copy-start.28 = (f32[4,256]{1,0:T(4,128)S(1)}, f32[4,256]{1,0:T(4,128)}, u32[]{:S(2)}) copy-start(f32[4,256]{1,0:T(4,128)} %copy-done.27) | copy-start | bytes 12292
  198.3 6.3 %copy-start.33 = (pred[4]{0:T(512)(128)(4,1)S(1)}, pred[4]{0:T(512)(128)(4,1)}, u32[]{:S(2)}) copy-start(pred[4]{0:T(512)(128)(4,1)} %get-tuple-element.55) | copy-start | bytes 16
  198.3 7.2 %copy-start.8 = (f32[4,64,64]{2,1,0:T(8,128)S(1)}, f32[4,64,64]{2,1,0:T(8,128)}, u32[]{:S(2)}) copy-start(f32[4,64,64]{2,1,0:T(8,128)} %param.14) | copy-start | bytes 196612
  198.3 7.2 %copy-start.12 = (f32[32,64]{1,0:T(8,128)S(1)}, f32[32,64]{1,0:T(8,128)}, u32[]{:S(2)}) copy-start(f32[32,64]{1,0:T(8,128)} %get-tuple-element.40) | copy-start | bytes 24580
  198.3 7.2 %copy-start.13 = (f32[32,64]{1,0:T(8,128)S(1)}, f32[32,64]{1,0:T(8,128)}, u32[]{:S(2)}) copy-start(f32[32,64]{1,0:T(8,128)} %get-tuple-element.41) | copy-start | bytes 24580
  (5 other events, 13.2 us)

commit v3 on v2

--- a/solution.py
+++ b/solution.py
@@ -38,16 +38,6 @@
 def unfold(values):
     half = values.shape[-1] // 2
     return jnp.concatenate([values[..., :half], values[..., half:]], axis=-2)
-
-
-def ring_events():
-    events = []
-    reach = SIDE // 2
-    for a in range(-reach, reach):
-        plus, minus = (reach, reach - 1) if a % 2 == 0 else (reach - 1, reach)
-        for b in range(-plus, minus + 1):
-            events.append((abs(a) + abs(b), abs(b), a, b, plus, minus))
-    return sorted(events)
 
 
 def place():
@@ -70,11 +60,16 @@
     row_ref,
     parts_ref,
     edges_ref,
+    where_ref,
+    source_ref,
+    parents_ref,
+    halo_ref,
     gather_ref,
-    halo_ref,
     sums_ref,
-    ring_send,
-    ring_recv,
+    near_send,
+    near_recv,
+    slab_send,
+    slab_recv,
     pair_send,
     pair_recv,
     small_send,
@@ -83,11 +78,17 @@
     y, z, core, sub = place()
     leaf = lax.axis_index("leaf")
     rank = skeleton_ref.shape[1]
+    reach = SIDE // 2
+    width = SIDE // 2
     partner = (leaf_of(y, z, 1 - core), sub)
-    y_up = (leaf_of(wrapped(y, 1, SIDE), z, core), sub)
-    y_down = (leaf_of(wrapped(y, -1, SIDE), z, core), sub)
-    z_up = (leaf_of(y, wrapped(z, 1, SIDE), core), sub)
-    z_down = (leaf_of(y, wrapped(z, -1, SIDE), core), sub)
+    y_ring = (
+        (leaf_of(wrapped(y, 1, SIDE), z, core), sub),
+        (leaf_of(wrapped(y, -1, SIDE), z, core), sub),
+    )
+    z_ring = (
+        (leaf_of(y, wrapped(z, 1, SIDE), core), sub),
+        (leaf_of(y, wrapped(z, -1, SIDE), core), sub),
+    )
     peers = [(leaf, wrapped(sub, step, subs)) for step in range(1, subs)]
     position = leaf * subs + sub
     total = leaf_total * subs
@@ -97,13 +98,20 @@
     before = (before // subs, before % subs)
 
     barrier = pltpu.get_barrier_semaphore()
-    others = [partner, y_up, y_down, z_up, z_down] + peers + [after, before]
+    others = [partner, *y_ring, *z_ring] + peers + [after, before]
     for other in others:
         pl.semaphore_signal(barrier, inc=1, device_id=other, device_id_type=MESH)
 
-    gather_ref[0, y, z, core, :rank] = skeleton_ref[0]
-    gather_ref[1, y, z, core, :rank] = skeleton_ref[1]
-    gather_ref[1, y, z, core, rank:] = row_ref[...]
+    inner, outer = (z, y), (y, z)
+    inner_ring, outer_ring = (z_ring, y_ring), (y_ring, z_ring)
+
+    def slot(half, a, b):
+        return (core * SIDE + wrapped(outer[half], b, SIDE)) * SIDE + wrapped(inner[half], a, SIDE)
+
+    own = (slot(0, 0, 0), slot(1, 0, 0))
+    gather_ref[0, own[0], :rank] = skeleton_ref[0]
+    gather_ref[1, own[1], :rank] = skeleton_ref[1]
+    gather_ref[1, own[1], rank:] = row_ref[...]
     pl.semaphore_wait(barrier, len(others))
 
     small = []
@@ -129,111 +137,158 @@
                 device_id_type=MESH,
             )
         )
-    for copy in small:
+    for copy in small[: subs - 1]:
         copy.start()
 
-    def block(half, a, b):
-        if half == 0:
-            return gather_ref.at[0, wrapped(y, b, SIDE), wrapped(z, a, SIDE), core]
-        return gather_ref.at[1, wrapped(y, a, SIDE), wrapped(z, b, SIDE), core]
-
-    first = ((z_up, z_down), (y_up, y_down))
-    second = ((y_up, y_down), (z_up, z_down))
-
-    def ring_copy(half, a, b, landed_a, landed_b, other):
-        i, j = landed_a % SIDE, landed_b % SIDE
-        here = block(half, a, b)
+    sent = []
+
+    def near_copy(half, a, way):
+        here = gather_ref.at[half, slot(half, a, 0)]
+        landed = (a - 1 if way == 0 else a + 1) % SIDE
         return pltpu.make_async_remote_copy(
             src_ref=here,
             dst_ref=here,
-            send_sem=ring_send.at[half, i, j],
-            recv_sem=ring_recv.at[half, i, j],
-            device_id=other,
+            send_sem=near_send.at[half, landed],
+            recv_sem=near_recv.at[half, landed],
+            device_id=inner_ring[half][way],
             device_id_type=MESH,
         )
 
-    def pair_copy(half, a, b):
-        here = block(half, a, b)
+    def slab(half, group, b):
+        first = (core * SIDE + wrapped(outer[half], b, SIDE)) * SIDE + group * width
+        return gather_ref.at[half, pl.ds(first, width)]
+
+    def slab_copy(half, group, b, way):
+        here = slab(half, group, b)
+        landed = (b - 1 if way == 0 else b + 1) % SIDE
         return pltpu.make_async_remote_copy(
             src_ref=here,
             dst_ref=here,
-            send_sem=pair_send.at[half, a % SIDE, b % SIDE],
-            recv_sem=pair_recv.at[half, a % SIDE, b % SIDE],
+            send_sem=slab_send.at[half, group, landed],
+            recv_sem=slab_recv.at[half, group, landed],
+            device_id=outer_ring[half][way],
+            device_id_type=MESH,
+        )
+
+    def pair_copy(half, group, b):
+        here = slab(half, group, b)
+        return pltpu.make_async_remote_copy(
+            src_ref=here,
+            dst_ref=here,
+            send_sem=pair_send.at[half, group, b % SIDE],
+            recv_sem=pair_recv.at[half, group, b % SIDE],
             device_id=partner,
             device_id_type=MESH,
         )
 
-    sent = []
-
-    def pass_on(half, a, b, plus, minus):
-        copies = []
-        up, down = first[half]
-        reach = SIDE // 2
-        if b == 0:
-            if -reach < a <= 0:
-                copies.append(ring_copy(half, a, b, a - 1, b, up))
-            if 0 <= a < reach - 1:
-                copies.append(ring_copy(half, a, b, a + 1, b, down))
-        up, down = second[half]
-        if -plus < b <= 0:
-            copies.append(ring_copy(half, a, b, a, b - 1, up))
-        if 0 <= b < minus:
-            copies.append(ring_copy(half, a, b, a, b + 1, down))
-        copies.append(pair_copy(half, a, b))
-        for copy in copies:
-            copy.start()
-        sent.extend(copies)
-
-    events = ring_events()
-    _, _, a, b, plus, minus = events[0]
-    pass_on(1, a, b, plus, minus)
+    def go(copy):
+        copy.start()
+        sent.append(copy)
+
+    for way in (0, 1):
+        go(near_copy(1, 0, way))
     for copy in small[: subs - 1]:
         copy.wait_recv()
     parent = parts_ref[sub]
     for step in range(subs - 1):
         parent = parent + sums_ref[step]
-    gather_ref[0, y, z, core, rank:] = parent
-    pass_on(0, a, b, plus, minus)
-    for _, _, a, b, plus, minus in events[1:]:
+    gather_ref[0, own[0], rank:] = parent
+    for copy in small[subs - 1 :]:
+        copy.start()
+    for way in (0, 1):
+        go(near_copy(0, 0, way))
+
+    def limit(group, way):
+        return reach if group == way else reach - 1
+
+    for step in range(1, reach + 1):
         for half in (1, 0):
-            ring_copy(half, a, b, a, b, partner).wait_recv()
-            pass_on(half, a, b, plus, minus)
+            for way in (0, 1):
+                if step <= reach - way:
+                    a = -step if way == 0 else step
+                    near_copy(half, a + 1 if way == 0 else a - 1, way).wait_recv()
+                    if step < reach - way:
+                        go(near_copy(half, a, way))
+            if step == reach:
+                for way in (0, 1):
+                    for group in (way, 1 - way):
+                        go(slab_copy(half, group, 0, way))
+                for group in (0, 1):
+                    go(pair_copy(half, group, 0))
+    for step in range(1, reach + 1):
+        for half in (1, 0):
+            for turn in (0, 1):
+                for way in (0, 1):
+                    group = way if turn == 0 else 1 - way
+                    if step > limit(group, way):
+                        continue
+                    b = -step if way == 0 else step
+                    slab_copy(half, group, b + 1 if way == 0 else b - 1, way).wait_recv()
+                    if step < limit(group, way):
+                        go(slab_copy(half, group, b, way))
+                    go(pair_copy(half, group, b))
     for copy in small:
         copy.wait_send()
     for copy in small[subs - 1 :]:
         copy.wait_recv()
+    for half in (1, 0):
+        for group in (0, 1):
+            for b in range(SIDE):
+                pair_copy(half, group, b).wait_recv()
+
+    plane = SIDE * SIDE
+    for side in range(CORES):
+        parents_ref[:, side] = gather_ref[0, side * plane : (side + 1) * plane, rank:]
+    leaves, entries = source_ref.shape[0], source_ref.shape[2] // rank
+    lane = lax.broadcasted_iota(jnp.int32, (rank, row_ref.shape[1]), 1)
+    for target in range(leaves):
+        for entry in range(entries):
+            at_0 = where_ref[0, target * entries + entry]
+            at_1 = where_ref[1, target * entries + entry]
+            low = gather_ref[0, at_0, :rank]
+            high = gather_ref[1, at_1, :rank]
+            named = jnp.broadcast_to(gather_ref[1, at_1, rank : rank + 1], lane.shape)
+            named = jnp.sum(jnp.where(lane == leaf, named, 0.0), axis=1, keepdims=True)
+            both = jnp.where(named < 1.5, low, high)
+            odd = (named == 1.0) | (named == 3.0)
+            source_ref[target, :, entry * rank : (entry + 1) * rank] = jnp.where(
+                odd, both[:, rank:], both[:, :rank]
+            )
     for copy in sent:
         copy.wait_send()
-    for _, _, a, b, _, _ in events:
-        for half in (0, 1):
-            pair_copy(half, a, b).wait_recv()
-
-
-def exchange(skeleton, row, parts, edges, subs, leaf_total):
-    rows = skeleton.shape[1] + row.shape[0]
+
+
+def exchange(skeleton, row, parts, edges, where, leaves, subs, leaf_total):
+    rank = skeleton.shape[1]
+    rows = rank + row.shape[0]
     lanes = skeleton.shape[2]
+    entries = where.shape[1] // leaves
     vmem = pl.BlockSpec(memory_space=pltpu.VMEM)
     dma = pltpu.SemaphoreType.DMA
     return pl.pallas_call(
         functools.partial(exchange_kernel, subs, leaf_total),
         out_shape=(
-            jax.ShapeDtypeStruct((2, SIDE, SIDE, CORES, rows, lanes), jnp.float32),
+            jax.ShapeDtypeStruct((leaves, rank, entries * rank), jnp.float32),
+            jax.ShapeDtypeStruct((leaf_total // CORES, CORES, row.shape[0], lanes), jnp.float32),
             jax.ShapeDtypeStruct(edges.shape, jnp.float32),
         ),
-        in_specs=[vmem] * 4,
-        out_specs=(vmem, vmem),
+        in_specs=[vmem] * 4 + [pl.BlockSpec(memory_space=pltpu.SMEM)],
+        out_specs=(vmem, vmem, vmem),
         scratch_shapes=[
+            pltpu.VMEM((2, leaf_total, rows, lanes), jnp.float32),
             pltpu.VMEM((subs - 1,) + parts.shape[1:], jnp.float32),
-            dma((2, SIDE, SIDE)),
-            dma((2, SIDE, SIDE)),
-            dma((2, SIDE, SIDE)),
-            dma((2, SIDE, SIDE)),
+            dma((2, SIDE)),
+            dma((2, SIDE)),
+            dma((2, 2, SIDE)),
+            dma((2, 2, SIDE)),
+            dma((2, 2, SIDE)),
+            dma((2, 2, SIDE)),
             dma((subs + 1,)),
             dma((subs + 1,)),
         ],
         compiler_params=pltpu.CompilerParams(collective_id=0, has_side_effects=True),
         name="exchange",
-    )(skeleton, row, parts, edges)
+    )(skeleton, row, parts, edges, where)
 
 
 def sum_kernel(subs, in_ref, out_ref, sums_ref, send_sem, recv_sem):
@@ -283,20 +338,18 @@
     )(values)
 
 
-def one_product(field, near_kernels, basis, up, down, couplings, top, row, slots, blocks):
+def one_product(field, near_kernels, basis, up, down, chosen, top, row, where):
     rhs, leaves, size = field.shape
     rank = basis.shape[1]
     subs = lax.axis_size("sub")
     leaf_total = lax.axis_size("leaf")
-    leaf = lax.axis_index("leaf")
     skeleton = jnp.einsum("pla,lra->lpr", field, basis, precision=precise)
     parent_t = jnp.einsum("lpr,lrq->qp", skeleton, up, precision=precise)
     parts = fold(parent_t.reshape(subs, rank // subs, rhs))
     pairs = jnp.concatenate([skeleton[0::2], skeleton[1::2]], axis=-1)
     edges = jnp.stack([field[:, 0], field[:, -1]])
-    gathered, sides = exchange(pairs, row, parts, edges, subs, leaf_total)
-    gathered = gathered.reshape(2, leaf_total, -1, 2 * rank)
-    parents = unfold(gathered[0, :, rhs:])
+    sources, parents, sides = exchange(pairs, row, parts, edges, where, leaves, subs, leaf_total)
+    parents = unfold(parents.reshape(leaf_total, -1, 2 * rank))
     top_part = jnp.einsum("erp,erq->pq", parents, top, precision=precise)
     top_term = unfold(sum_over_sub(fold(top_part), subs))
     padded = jnp.concatenate([sides[0][:, None], field, sides[1][:, None]], axis=1)
@@ -305,11 +358,7 @@
         near = near + jnp.einsum(
             "plb,lba->pla", padded[:, side : side + leaves], near_kernels[side], precision=precise
         )
-    chosen = lax.dynamic_index_in_dim(gathered[1, :, rhs], leaf, 1, keepdims=False)[slots]
-    chosen = chosen.astype(jnp.int32)
-    both = gathered[chosen // 2, slots, :rhs]
-    source = jnp.where((chosen % 2 == 0)[..., None, None], both[..., :rank], both[..., rank:])
-    far = jnp.einsum("lkpr,lkrq->lpq", source, couplings[blocks], precision=precise)
+    far = jnp.einsum("lpm,lmq->lpq", sources, chosen, precision=precise)
     coef = far + jnp.einsum("pr,lrq->lpq", top_term, down, precision=precise)
     return near + jnp.einsum("lpr,lra->pla", coef, basis, precision=precise)
 
@@ -331,6 +380,13 @@
         values = kernel_blocks(all_points[:, side : side + leaves], points, size)
         near_kernels.append(jnp.where(present[:, None, None], values, 0.0))
     row = jnp.broadcast_to(send_leaf.reshape(1, -1).astype(jnp.float32), (8, send_leaf.size))
+    rank = basis.shape[1]
+    chosen = couplings[list_block].reshape(leaves, -1, rank)
+    flat = list_slot.reshape(-1)
+    slot_y, slot_z, slot_core = flat // (SIDE * CORES), (flat // CORES) % SIDE, flat % CORES
+    where = jnp.stack(
+        [(slot_core * SIDE + slot_y) * SIDE + slot_z, (slot_core * SIDE + slot_z) * SIDE + slot_y]
+    )
     current = field.reshape(rhs, leaves, size)
     for repeat in range(2):
         current = one_product(
@@ -339,11 +395,10 @@
             basis,
             up_transfer,
             down_transfer,
-            couplings,
+            chosen,
             top_coupling[0],
             row,
-            list_slot,
-            list_block,
+            where,
         )
     return current.reshape(rhs, leaves * size)
 

time: 208 us -> 182 us (0.88)
  local copies, waits for them, and re-layouts: 47.9 us -> 22.8 us
  Pallas kernels: 122 us -> 130 us
  matrix products: 18.7 us -> 13.2 us
  other arithmetic: 9.96 us -> 7.3 us
    reshape x2 -> x1, local copies, waits for them, and re-layouts: 18.4 us -> 0.08 us  [local(): flat = list_slot.reshape(-1)]
    gather x5 -> x1, local copies, waits for them, and re-layouts: 8.46 us -> 0.61 us  [local(): chosen = couplings[list_block].reshape(leaves, -1, rank)]
    pallas_call x2, Pallas kernels: 109 us -> 114 us  [exchange(): pl.pallas_call(functools.partial(exchange_kernel, subs, leaf_total), out_...]
    unnamed x74 -> x92, local copies, waits for them, and re-layouts: 2.26 us -> 6.76 us
    slice x4 -> x0, local copies, waits for them, and re-layouts: 4.31 us -> none  [the longest x2 2.15 us: one_product(): parents = unfold(gathered[0, :, rhs:])]
    dot_general x6, matrix products: 10.6 us -> 7.52 us  [one_product(): jnp.einsum('plb,lba->pla', padded[:, side:side + leaves], near_kernels[si...]
    pallas_call x2, Pallas kernels: 12.7 us -> 15.3 us  [sum_over_sub(): pl.pallas_call(functools.partial(sum_kernel, subs), out_shape=jax.ShapeDt...]
    sub x3, local copies, waits for them, and re-layouts: 0.7 us -> 3.14 us  [kernel_blocks(): gap = sources[component][:, :, None] - targets[component][:, None, :]]
  transfers between devices with their start and end apart: 2 -> 2, of which waited for: 0 -> 0; matrix products, arithmetic and copies ran while one was open for 16% -> 11% of each run, Pallas kernels for 32% -> 39%
where the time goes in v3:
time: 182 us; the launch traced here: 181 us
  Pallas kernels  130 us (71%)
  local copies, waits for them, and re-layouts  22.8 us (13%)
  matrix products  13.2 us (7%)
  starting transfers between devices  7.69 us (4%)
  other arithmetic  7.3 us (4%)
    pallas_call x2, Pallas kernels, exchange(): pl.pallas_call(functools.partial(exchange_kernel, subs, leaf_total), out_...  114 us
    pallas_call x2, Pallas kernels, sum_over_sub(): pl.pallas_call(functools.partial(sum_kernel, subs), out_shape=jax.ShapeDt...  15.3 us
    dot_general x6, matrix products, one_product(): jnp.einsum('plb,lba->pla', padded[:, side:side + leaves], near_kernels[si...  7.52 us
    unnamed x92, local copies, waits for them, and re-layouts  6.76 us
    ppermute x1, starting transfers between devices, halo(): high = lax.ppermute(block[:, 0], axes, backward)  5.77 us
    slice x4, local copies, waits for them, and re-layouts, unfold(): return jnp.concatenate([values[..., :half], values[..., half:]], axis=-2)  3.96 us
  transfers between devices with their start and end apart: 2, of which 0 were waited for; matrix products, arithmetic and copies ran while one was open for 11% of the time, Pallas kernels for 39%

profile of v3, /device:TPU:1, one launch (start us, length us, event | category | flops | bytes accessed | tf_op | source)
XLA Modules:
  0.0 181.2 jit_solution(4736310239475191087)
XLA Ops:
  0.0 1.4 slice_bitcast_fusion.8
  1.4 5.8 %collective-permute-start.1 = (f32[3,256]{1,0:T(4,128)}, f32[3,256]{1,0:T(4,128)}, u32[]{:S(2)}, u32[]{:S(2)}) collective-permute-start(f32[3,256]{1,0:T(4,128)} %get-tuple-element.52), channel_id=1, source_target_pairs={{1,0},{2,1},{3,2},{4,3},{5,4},{6,5},{7,6},{8,7},{9,8},{10,9},{11,1... | collective-permute-start | bytes 9224 | tf_op jit(solution)/shard_map/ppermute | solution.py:21
  7.2 1.9 %collective-permute-start = (f32[3,256]{1,0:T(4,128)}, f32[3,256]{1,0:T(4,128)}, u32[]{:S(2)}, u32[]{:S(2)}) collective-permute-start(f32[3,256]{1,0:T(4,128)} %get-tuple-element.53), channel_id=1, source_target_pairs={{0,1},{1,2},{2,3},{3,4},{4,5},{5,6},{6,7},{7,8},{8,9},{9,10},{10,1... | collective-permute-start | bytes 9224 | tf_op jit(solution)/shard_map/ppermute | solution.py:20
  11.3 1.0 copy.43
  12.7 0.9 copy-done.9
  15.2 0.7 pad_maximum_fusion.10.skeleton_ref
  15.9 0.7 pad_maximum_fusion.8.edges_ref
  17.2 62.9 %exchange.2 = (f32[4,64,512]{2,1,0:T(8,128)}, f32[64,2,8,128]{3,2,1,0:T(8,128)}, f32[2,64,256]{2,1,0:T(8,128)}) custom-call(f32[2,64,128]{2,1,0:T(8,128)} %pad_maximum_fusion.10.skeleton_ref, f32[8,128]{1,0:T(8,128)} %broadcast_in_dim.44.row_ref, f32[4,8,128]{2,1,0:T(8,128)} %pad_maximum_fusion.12.parts_ref, f32[2,64,256]{2,1,0:T(8,128)} %pad_maximum_fusion.8.edges_ref, ...), custom_call_target="tpu_custom_call" | custom-call | tf_op jit(solution)/shard_map/exchange/pallas_call | solution.py:268
  80.2 1.5 slice_bitcast_fusion.6
  81.7 1.4 fusion.118
  83.6 0.8 copy-done.2
  85.5 8.3 %sum_over_sub.2 = f32[32,128]{1,0:T(8,128)} custom-call(f32[32,128]{1,0:T(8,128)} %pad_maximum_fusion.13.in_ref), custom_call_target="tpu_custom_call" | custom-call | tf_op jit(solution)/shard_map/sum_over_sub/pallas_call | solution.py:326
  93.8 1.5 fusion.126
  95.9 1.5 fusion.127
  98.9 1.3 sub.135
  100.2 1.3 sub.145
  102.1 0.7 broadcast_in_dim.47
  102.8 0.7 broadcast_in_dim.42
  104.1 1.7 fusion.8
  105.9 1.3 convolution_add_fusion.3
  107.9 0.9 fusion.4
  109.4 0.7 copy-done.10
  110.5 0.7 pad_maximum_fusion.14.parts_ref
  111.2 0.7 pad_maximum_fusion.11.skeleton_ref
  112.6 51.3 %exchange.3 = (f32[4,64,512]{2,1,0:T(8,128)}, f32[64,2,8,128]{3,2,1,0:T(8,128)}, f32[2,64,256]{2,1,0:T(8,128)}) custom-call(f32[2,64,128]{2,1,0:T(8,128)} %pad_maximum_fusion.11.skeleton_ref, f32[8,128]{1,0:T(8,128)} %broadcast_in_dim.44.row_ref, f32[4,8,128]{2,1,0:T(8,128)} %pad_maximum_fusion.14.parts_ref, f32[2,64,256]{2,1,0:T(8,128)} %pad_maximum_fusion.9.edges_ref, ...), custom_call_target="tpu_custom_call" | custom-call | tf_op jit(solution)/shard_map/exchange/pallas_call | solution.py:268
  163.9 1.5 fusion.129
  166.1 1.0 fusion.7
  167.1 1.7 convolution_add_fusion.1
  170.5 7.0 %sum_over_sub.3 = f32[32,128]{1,0:T(8,128)} custom-call(f32[32,128]{1,0:T(8,128)} %pad_maximum_fusion.15.in_ref), custom_call_target="tpu_custom_call" | custom-call | tf_op jit(solution)/shard_map/sum_over_sub/pallas_call | solution.py:326
  177.5 0.9 fusion.125
  179.1 0.9 fusion.3
  180.5 0.7 copy.39
  (133 shorter events, 15.1 us)
Async XLA Ops:
  0.0 95.3 %copy-start = (f32[32,64,64]{2,1,0:T(8,128)S(1)}, f32[32,64,64]{2,1,0:T(8,128)}, u32[]{:S(2)}) copy-start(f32[32,64,64]{2,1,0:T(8,128)} %param.15) | copy-start | bytes 1572868
  0.0 9.1 %copy-start.14 = (f32[3,1024]{1,0:T(4,128)S(1)}, f32[3,1024]{1,0:T(4,128)}, u32[]{:S(2)}) copy-start(f32[3,1024]{1,0:T(4,128)} %param.11) | copy-start | bytes 36868
  1.4 100.6 %collective-permute-start.1 = (f32[3,256]{1,0:T(4,128)}, f32[3,256]{1,0:T(4,128)}, u32[]{:S(2)}, u32[]{:S(2)}) collective-permute-start(f32[3,256]{1,0:T(4,128)} %get-tuple-element.52), channel_id=1, source_target_pairs={{1,0},{2,1},{3,2},{4,3},{5,4},{6,5},{7,6},{8,7},{9,8},{10,9},{11,1... | collective-permute-start | bytes 9224 | tf_op jit(solution)/shard_map/ppermute | solution.py:21
  7.2 95.6 %collective-permute-start = (f32[3,256]{1,0:T(4,128)}, f32[3,256]{1,0:T(4,128)}, u32[]{:S(2)}, u32[]{:S(2)}) collective-permute-start(f32[3,256]{1,0:T(4,128)} %get-tuple-element.53), channel_id=1, source_target_pairs={{0,1},{1,2},{2,3},{3,4},{4,5},{5,6},{6,7},{7,8},{8,9},{9,10},{10,1... | collective-permute-start | bytes 9224 | tf_op jit(solution)/shard_map/ppermute | solution.py:20
  11.3 1.1 copy-start.1
  11.3 1.1 copy-start.6
  12.4 1.5 copy-start.7
  83.4 1.1 copy-start.2
  95.9 1.6 copy-start.11
  95.9 1.6 copy-start.17
  95.9 1.6 copy-start.18
  97.5 6.0 %copy-start.8 = (f32[8,4,8,256]{3,2,0,1:T(8,128)S(1)}, f32[8,4,8,256]{3,2,0,1:T(8,128)}, u32[]{:S(2)}) copy-start(f32[8,4,8,256]{3,2,0,1:T(8,128)} %copy-done.7) | copy-start | bytes 786436
  100.2 1.3 copy-start.20
  100.2 3.3 %copy-start.19 = (f32[3,4,256]{2,1,0:T(4,128)S(1)}, f32[3,4,256]{2,1,0:T(4,128)}, u32[]{:S(2)}) copy-start(f32[3,4,256]{2,1,0:T(4,128)} %reshape.271) | copy-start | bytes 36868
  102.1 1.5 copy-start.16
  103.5 2.4 %copy-start.28 = (f32[4,256]{1,0:T(4,128)}, f32[4,256]{1,0:T(4,128)S(1)}, u32[]{:S(2)}) copy-start(f32[4,256]{1,0:T(4,128)S(1)} %get-tuple-element.60) | copy-start | bytes 12292
  103.5 2.4 %copy-start.30 = (f32[4,256]{1,0:T(4,128)}, f32[4,256]{1,0:T(4,128)S(1)}, u32[]{:S(2)}) copy-start(f32[4,256]{1,0:T(4,128)S(1)} %get-tuple-element.61) | copy-start | bytes 12292
  103.5 2.4 %copy-start.32 = (f32[4,256]{1,0:T(4,128)}, f32[4,256]{1,0:T(4,128)S(1)}, u32[]{:S(2)}) copy-start(f32[4,256]{1,0:T(4,128)S(1)} %get-tuple-element.62) | copy-start | bytes 12292
  103.5 3.8 %copy-start.24 = (f32[4,256]{1,0:T(4,128)}, f32[4,256]{1,0:T(4,128)S(1)}, u32[]{:S(2)}) copy-start(f32[4,256]{1,0:T(4,128)S(1)} %get-tuple-element.55) | copy-start | bytes 12292
  103.5 3.8 %copy-start.26 = (f32[4,256]{1,0:T(4,128)}, f32[4,256]{1,0:T(4,128)S(1)}, u32[]{:S(2)}) copy-start(f32[4,256]{1,0:T(4,128)S(1)} %get-tuple-element.56) | copy-start | bytes 12292
  104.1 1.7 copy-start.21
  104.1 1.7 copy-start.22
  104.1 1.7 copy-start.23
  104.1 1.7 copy-start.41
  105.9 1.4 copy-start.15
  109.1 58.0 %copy-start.4 = (f32[64,4,256]{2,0,1:T(8,128)}, f32[64,4,256]{2,0,1:T(8,128)S(1)}, u32[]{:S(2)}) copy-start(f32[64,4,256]{2,0,1:T(8,128)S(1)} %fusion.2) | copy-start | bytes 786436
  109.1 1.0 copy-start.10
  163.9 1.5 copy-start.13
  166.1 1.0 copy-start.42
  167.1 1.7 copy-start.3
  169.4 9.0 %copy-start.5 = (f32[64,4,256]{2,0,1:T(8,128)S(1)}, f32[64,4,256]{2,0,1:T(8,128)}, u32[]{:S(2)}) copy-start(f32[64,4,256]{2,0,1:T(8,128)} %copy-done.4) | copy-start | bytes 786436
  169.4 9.0 %copy-start.43 = (f32[4,256,64]{1,2,0:T(8,128)S(1)}, f32[4,256,64]{1,2,0:T(8,128)}, u32[]{:S(2)}) copy-start(f32[4,256,64]{1,2,0:T(8,128)} %convolution_add_fusion.1) | copy-start | bytes 786436
  (14 other events, 10.4 us)

commit v4 on v3

--- a/solution.py
+++ b/solution.py
@@ -12,14 +12,6 @@
 MESH = pl.DeviceIdType.MESH
 SIDE = 8
 CORES = 2
-
-
-def halo(block, axes, count):
-    forward = [(i, i + 1) for i in range(count - 1)]
-    backward = [(target, source) for source, target in forward]
-    low = lax.ppermute(block[:, -1], axes, forward)
-    high = lax.ppermute(block[:, 0], axes, backward)
-    return jnp.concatenate([low[:, None], block, high[:, None]], axis=1)
 
 
 def kernel_blocks(sources, targets, leaf_size):
@@ -81,14 +73,8 @@
     reach = SIDE // 2
     width = SIDE // 2
     partner = (leaf_of(y, z, 1 - core), sub)
-    y_ring = (
-        (leaf_of(wrapped(y, 1, SIDE), z, core), sub),
-        (leaf_of(wrapped(y, -1, SIDE), z, core), sub),
-    )
-    z_ring = (
-        (leaf_of(y, wrapped(z, 1, SIDE), core), sub),
-        (leaf_of(y, wrapped(z, -1, SIDE), core), sub),
-    )
+    y_line = [(leaf_of(wrapped(y, step, SIDE), z, core), sub) for step in range(1, SIDE)]
+    z_line = [(leaf_of(y, wrapped(z, step, SIDE), core), sub) for step in range(1, SIDE)]
     peers = [(leaf, wrapped(sub, step, subs)) for step in range(1, subs)]
     position = leaf * subs + sub
     total = leaf_total * subs
@@ -98,12 +84,13 @@
     before = (before // subs, before % subs)
 
     barrier = pltpu.get_barrier_semaphore()
-    others = [partner, *y_ring, *z_ring] + peers + [after, before]
+    others = [partner] + y_line + z_line + peers + [after, before]
     for other in others:
         pl.semaphore_signal(barrier, inc=1, device_id=other, device_id_type=MESH)
 
     inner, outer = (z, y), (y, z)
-    inner_ring, outer_ring = (z_ring, y_ring), (y_ring, z_ring)
+    inner_line = (z_line, y_line)
+    outer_ring = ((y_line[0], y_line[-1]), (z_line[0], z_line[-1]))
 
     def slot(half, a, b):
         return (core * SIDE + wrapped(outer[half], b, SIDE)) * SIDE + wrapped(inner[half], a, SIDE)
@@ -142,17 +129,26 @@
 
     sent = []
 
-    def near_copy(half, a, way):
-        here = gather_ref.at[half, slot(half, a, 0)]
-        landed = (a - 1 if way == 0 else a + 1) % SIDE
+    def near_copy(half, step):
+        here = gather_ref.at[half, own[half]]
         return pltpu.make_async_remote_copy(
             src_ref=here,
             dst_ref=here,
-            send_sem=near_send.at[half, landed],
-            recv_sem=near_recv.at[half, landed],
-            device_id=inner_ring[half][way],
+            send_sem=near_send.at[half, step],
+            recv_sem=near_recv.at[half, step],
+            device_id=inner_line[half][step - 1],
             device_id_type=MESH,
         )
+
+    def near_wait(half, step):
+        pltpu.make_async_remote_copy(
+            src_ref=gather_ref.at[half, own[half]],
+            dst_ref=gather_ref.at[half, slot(half, -step, 0)],
+            send_sem=near_send.at[half, step],
+            recv_sem=near_recv.at[half, step],
+            device_id=inner_line[half][step - 1],
+            device_id_type=MESH,
+        ).wait_recv()
 
     def slab(half, group, b):
         first = (core * SIDE + wrapped(outer[half], b, SIDE)) * SIDE + group * width
@@ -185,8 +181,9 @@
         copy.start()
         sent.append(copy)
 
-    for way in (0, 1):
-        go(near_copy(1, 0, way))
+    order = sorted(range(1, SIDE), key=lambda step: -min(step, SIDE - step))
+    for step in order:
+        go(near_copy(1, step))
     for copy in small[: subs - 1]:
         copy.wait_recv()
     parent = parts_ref[sub]
@@ -195,26 +192,20 @@
     gather_ref[0, own[0], rank:] = parent
     for copy in small[subs - 1 :]:
         copy.start()
-    for way in (0, 1):
-        go(near_copy(0, 0, way))
+    for step in order:
+        go(near_copy(0, step))
 
     def limit(group, way):
         return reach if group == way else reach - 1
 
-    for step in range(1, reach + 1):
-        for half in (1, 0):
-            for way in (0, 1):
-                if step <= reach - way:
-                    a = -step if way == 0 else step
-                    near_copy(half, a + 1 if way == 0 else a - 1, way).wait_recv()
-                    if step < reach - way:
-                        go(near_copy(half, a, way))
-            if step == reach:
-                for way in (0, 1):
-                    for group in (way, 1 - way):
-                        go(slab_copy(half, group, 0, way))
-                for group in (0, 1):
-                    go(pair_copy(half, group, 0))
+    for half in (1, 0):
+        for step in range(1, SIDE):
+            near_wait(half, step)
+        for way in (0, 1):
+            for group in (way, 1 - way):
+                go(slab_copy(half, group, 0, way))
+        for group in (0, 1):
+            go(pair_copy(half, group, 0))
     for step in range(1, reach + 1):
         for half in (1, 0):
             for turn in (0, 1):
@@ -338,7 +329,22 @@
     )(values)
 
 
-def one_product(field, near_kernels, basis, up, down, chosen, top, row, where):
+def build_near(points, sides):
+    leaves, size = points.shape[1:]
+    subs = lax.axis_size("sub")
+    total = lax.axis_size("leaf") * subs * leaves
+    position = lax.axis_index("leaf") * subs + lax.axis_index("sub")
+    all_points = jnp.concatenate([sides[0][:, None], points, sides[1][:, None]], axis=1)
+    near_kernels = []
+    for side in range(3):
+        index = position * leaves + jnp.arange(leaves) + (side - 1)
+        present = (index >= 0) & (index < total)
+        values = kernel_blocks(all_points[:, side : side + leaves], points, size)
+        near_kernels.append(jnp.where(present[:, None, None], values, 0.0))
+    return near_kernels
+
+
+def one_product(field, points, near_kernels, basis, up, down, chosen, top, row, where):
     rhs, leaves, size = field.shape
     rank = basis.shape[1]
     subs = lax.axis_size("sub")
@@ -348,11 +354,14 @@
     parts = fold(parent_t.reshape(subs, rank // subs, rhs))
     pairs = jnp.concatenate([skeleton[0::2], skeleton[1::2]], axis=-1)
     edges = jnp.stack([field[:, 0], field[:, -1]])
+    edges = jnp.concatenate([edges, jnp.stack([points[:, 0], points[:, -1]])], axis=1)
     sources, parents, sides = exchange(pairs, row, parts, edges, where, leaves, subs, leaf_total)
     parents = unfold(parents.reshape(leaf_total, -1, 2 * rank))
     top_part = jnp.einsum("erp,erq->pq", parents, top, precision=precise)
     top_term = unfold(sum_over_sub(fold(top_part), subs))
-    padded = jnp.concatenate([sides[0][:, None], field, sides[1][:, None]], axis=1)
+    padded = jnp.concatenate([sides[0, :rhs, None], field, sides[1, :rhs, None]], axis=1)
+    if near_kernels is None:
+        near_kernels = build_near(points, sides[:, rhs:])
     near = 0.0
     for side in range(3):
         near = near + jnp.einsum(
@@ -360,7 +369,7 @@
         )
     far = jnp.einsum("lpm,lmq->lpq", sources, chosen, precision=precise)
     coef = far + jnp.einsum("pr,lrq->lpq", top_term, down, precision=precise)
-    return near + jnp.einsum("lpr,lra->pla", coef, basis, precision=precise)
+    return near + jnp.einsum("lpr,lra->pla", coef, basis, precision=precise), near_kernels
 
 
 def local(
@@ -368,17 +377,8 @@
 ):
     rhs = field.shape[0]
     leaves, _, size = basis.shape
-    subs = lax.axis_size("sub")
-    count = lax.axis_size("leaf") * subs
-    position = lax.axis_index("leaf") * subs + lax.axis_index("sub")
-    points = coords.reshape(3, leaves, size)
-    all_points = halo(points, ("leaf", "sub"), count)
-    near_kernels = []
-    for side in range(3):
-        index = position * leaves + jnp.arange(leaves) + (side - 1)
-        present = (index >= 0) & (index < count * leaves)
-        values = kernel_blocks(all_points[:, side : side + leaves], points, size)
-        near_kernels.append(jnp.where(present[:, None, None], values, 0.0))
+    points = jnp.pad(coords, ((0, 5), (0, 0))).reshape(8, leaves, size)
+    near_kernels = None
     row = jnp.broadcast_to(send_leaf.reshape(1, -1).astype(jnp.float32), (8, send_leaf.size))
     rank = basis.shape[1]
     chosen = couplings[list_block].reshape(leaves, -1, rank)
@@ -389,8 +389,9 @@
     )
     current = field.reshape(rhs, leaves, size)
     for repeat in range(2):
-        current = one_product(
+        current, near_kernels = one_product(
             current,
+            points,
             near_kernels,
             basis,
             up_transfer,

time: 182 us -> 157 us (0.86)
  local copies, waits for them, and re-layouts: 22.8 us -> 12.9 us
  Pallas kernels: 130 us -> 122 us
  starting transfers between devices: 7.69 us -> 0 us
    ppermute x2 -> x0, starting transfers between devices: 7.69 us -> none  [the longest x1 5.77 us: halo(): high = lax.ppermute(block[:, 0], axes, backward)]
    pallas_call x2, Pallas kernels: 114 us -> 109 us  [exchange(): pl.pallas_call(functools.partial(exchange_kernel, subs, leaf_total), out_...]
    sub x3, local copies, waits for them, and re-layouts: 3.14 us -> 0.03 us  [kernel_blocks(): gap = sources[component][:, :, None] - targets[component][:, None, :]]
    pallas_call x2, Pallas kernels: 15.3 us -> 13.2 us  [sum_over_sub(): pl.pallas_call(functools.partial(sum_kernel, subs), out_shape=jax.ShapeDt...]
    unnamed x92 -> x91, local copies, waits for them, and re-layouts: 6.76 us -> 5.42 us
  transfers between devices with their start and end apart: 2 -> 0, of which waited for: 0 -> 0; matrix products, arithmetic and copies ran while one was open for 11% -> 0% of each run, Pallas kernels for 39% -> 0%
where the time goes in v4:
time: 157 us; the launch traced here: 156 us
  Pallas kernels  122 us (78%)
  matrix products  14 us (9%)
  local copies, waits for them, and re-layouts  12.9 us (8%)
  other arithmetic  6.09 us (4%)
    pallas_call x2, Pallas kernels, exchange(): pl.pallas_call(functools.partial(exchange_kernel, subs, leaf_total), out_...  109 us
    pallas_call x2, Pallas kernels, sum_over_sub(): pl.pallas_call(functools.partial(sum_kernel, subs), out_shape=jax.ShapeDt...  13.2 us
    dot_general x6, matrix products, one_product(): jnp.einsum('plb,lba->pla', padded[:, side:side + leaves], near_kernels[si...  7.74 us
    unnamed x91, local copies, waits for them, and re-layouts  5.42 us

profile of v4, /device:TPU:1, one launch (start us, length us, event | category | flops | bytes accessed | tf_op | source)
XLA Modules:
  0.0 156.2 jit_solution(15161756595719707419)
XLA Ops:
  0.0 0.7 copy-done.35
  2.4 1.3 fusion.115
  4.1 0.7 pad_maximum_fusion.11.parts_ref
  4.8 0.7 pad_maximum_fusion.9.skeleton_ref
  5.5 0.7 fusion.82.edges_ref
  6.2 59.7 %exchange.2 = (f32[4,64,512]{2,1,0:T(8,128)}, f32[64,2,8,128]{3,2,1,0:T(8,128)}, f32[2,72,256]{2,1,0:T(8,128)}) custom-call(f32[2,64,128]{2,1,0:T(8,128)} %pad_maximum_fusion.9.skeleton_ref, f32[8,128]{1,0:T(8,128)} %broadcast_in_dim.36.row_ref, f32[4,8,128]{2,1,0:T(8,128)} %pad_maximum_fusion.11.parts_ref, f32[2,72,256]{2,1,0:T(8,128)} %fusion.82.edges_ref, ...), custom_call_target="tpu_custom_call" | custom-call | tf_op jit(solution)/shard_map/exchange/pallas_call | solution.py:259
  65.9 0.7 slice_bitcast_fusion.10
  66.6 0.9 slice_bitcast_fusion.6
  68.1 1.0 fusion.8
  69.1 1.3 convolution_add_fusion.3
  70.5 1.7 %fusion.4 = f32[64,4,256]{2,0,1:T(8,128)} fusion(f32[4,256,64]{1,2,0:T(8,128)S(1)} %convolution_add_fusion.3, f32[4,256]{1,0:T(4,128)S(1)} %get-tuple-element.65, f32[4,256]{1,0:T(4,128)S(1)} %get-tuple-element.66, f32[4,256]{1,0:T(4,128)S(1)} %get-tuple-element.67, f32[4,256]{1,0:T(4,128)S(1)} %sub.147, f32[4,256]{1,0:T(4,128)S(1)} %sub.142, ...), kind=kOutput, calls=%fused_computation.10 | convolution fusion | flops 103677952 | bytes 876548 | tf_op jit(solution)/shard_map/plb,lba->pla/dot_general | solution.py:367
  72.8 0.8 copy-done.2
  74.0 0.7 pad_maximum_fusion.12.in_ref
  74.7 6.6 %sum_over_sub.2 = f32[32,128]{1,0:T(8,128)} custom-call(f32[32,128]{1,0:T(8,128)} %pad_maximum_fusion.12.in_ref), custom_call_target="tpu_custom_call" | custom-call | tf_op jit(solution)/shard_map/sum_over_sub/pallas_call | solution.py:317
  81.3 1.5 fusion.126
  82.7 0.6 gather_fusion
  84.9 0.8 copy-done.1
  86.2 0.9 convolution_bitcast_fusion.5
  87.1 0.8 copy.26
  87.9 0.7 pad_maximum_fusion.13.parts_ref
  88.6 0.7 pad_maximum_fusion.10.skeleton_ref
  89.3 0.7 fusion.81.edges_ref
  90.0 49.6 %exchange.3 = (f32[4,64,512]{2,1,0:T(8,128)}, f32[64,2,8,128]{3,2,1,0:T(8,128)}, f32[2,72,256]{2,1,0:T(8,128)}) custom-call(f32[2,64,128]{2,1,0:T(8,128)} %pad_maximum_fusion.10.skeleton_ref, f32[8,128]{1,0:T(8,128)} %broadcast_in_dim.36.row_ref, f32[4,8,128]{2,1,0:T(8,128)} %pad_maximum_fusion.13.parts_ref, f32[2,72,256]{2,1,0:T(8,128)} %fusion.81.edges_ref, ...), custom_call_target="tpu_custom_call" | custom-call | tf_op jit(solution)/shard_map/exchange/pallas_call | solution.py:259
  139.6 1.5 fusion.129
  141.2 0.6 copy-done.16
  141.9 1.0 fusion.7
  142.9 1.2 convolution_add_fusion.1
  144.1 1.7 %fusion.3 = f32[64,4,256]{2,0,1:T(8,128)} fusion(f32[4,256,64]{1,2,0:T(8,128)S(1)} %convolution_add_fusion.1, f32[4,256]{1,0:T(4,128)S(1)} %copy-done.24, f32[4,256]{1,0:T(4,128)S(1)} %copy-done.26, f32[4,256]{1,0:T(4,128)S(1)} %copy-done.22, f32[4,256]{1,0:T(4,128)S(1)} %copy-done.18, f32[4,256]{1,0:T(4,128)S(1)} %copy-done.20, ...), kind=kOutput, calls=%fused_computation.7 | convolution fusion | flops 103677952 | bytes 876548 | tf_op jit(solution)/shard_map/plb,lba->pla/dot_general | solution.py:367
  146.8 0.7 pad_maximum_fusion.14.in_ref
  147.5 6.6 %sum_over_sub.3 = f32[32,128]{1,0:T(8,128)} custom-call(f32[32,128]{1,0:T(8,128)} %pad_maximum_fusion.14.in_ref), custom_call_target="tpu_custom_call" | custom-call | tf_op jit(solution)/shard_map/sum_over_sub/pallas_call | solution.py:317
  154.1 0.9 fusion.125
  155.4 0.7 copy.41
  (127 shorter events, 7.1 us)
Async XLA Ops:
  0.0 82.7 %copy-start = (f32[32,64,64]{2,1,0:T(8,128)S(1)}, f32[32,64,64]{2,1,0:T(8,128)}, u32[]{:S(2)}) copy-start(f32[32,64,64]{2,1,0:T(8,128)} %param.15) | copy-start | bytes 1572868
  0.0 0.8 copy-start.33
  0.7 66.9 %copy-start.40 = (pred[4]{0:T(512)(128)(4,1)}, pred[4]{0:T(512)(128)(4,1)S(1)}, u32[]{:S(2)}) copy-start(pred[4]{0:T(512)(128)(4,1)S(1)} %compare_and_fusion.2) | copy-start | bytes 16
  0.9 68.2 %copy-start.38 = (pred[4]{0:T(512)(128)(4,1)}, pred[4]{0:T(512)(128)(4,1)S(1)}, u32[]{:S(2)}) copy-start(pred[4]{0:T(512)(128)(4,1)S(1)} %get-tuple-element.72) | copy-start | bytes 16
  0.9 69.6 %copy-start.36 = (pred[4]{0:T(512)(128)(4,1)}, pred[4]{0:T(512)(128)(4,1)S(1)}, u32[]{:S(2)}) copy-start(pred[4]{0:T(512)(128)(4,1)S(1)} %get-tuple-element.71) | copy-start | bytes 16
  0.9 1.4 copy-start.14
  2.3 68.1 %copy-start.15 = (f32[4,256]{1,0:T(4,128)}, f32[4,256]{1,0:T(4,128)S(1)}, u32[]{:S(2)}) copy-start(f32[4,256]{1,0:T(4,128)S(1)} %sub.137) | copy-start | bytes 12292
  2.3 68.1 %copy-start.17 = (f32[4,256]{1,0:T(4,128)}, f32[4,256]{1,0:T(4,128)S(1)}, u32[]{:S(2)}) copy-start(f32[4,256]{1,0:T(4,128)S(1)} %sub.147) | copy-start | bytes 12292
  2.4 68.1 %copy-start.19 = (f32[4,256]{1,0:T(4,128)}, f32[4,256]{1,0:T(4,128)S(1)}, u32[]{:S(2)}) copy-start(f32[4,256]{1,0:T(4,128)S(1)} %sub.142) | copy-start | bytes 12292
  2.4 1.3 copy-start.7
  4.1 1.4 copy-start.5
  67.5 3.0 %copy-start.21 = (f32[4,256]{1,0:T(4,128)}, f32[4,256]{1,0:T(4,128)S(1)}, u32[]{:S(2)}) copy-start(f32[4,256]{1,0:T(4,128)S(1)} %get-tuple-element.67) | copy-start | bytes 12292
  67.6 2.9 %copy-start.23 = (f32[4,256]{1,0:T(4,128)}, f32[4,256]{1,0:T(4,128)S(1)}, u32[]{:S(2)}) copy-start(f32[4,256]{1,0:T(4,128)S(1)} %get-tuple-element.65) | copy-start | bytes 12292
  67.6 2.9 %copy-start.25 = (f32[4,256]{1,0:T(4,128)}, f32[4,256]{1,0:T(4,128)S(1)}, u32[]{:S(2)}) copy-start(f32[4,256]{1,0:T(4,128)S(1)} %get-tuple-element.66) | copy-start | bytes 12292
  67.6 1.5 copy-start.29
  67.6 1.5 copy-start.31
  70.5 1.7 %copy-start.3 = (f32[64,2,8,128]{3,2,1,0:T(8,128)S(1)}, f32[64,2,8,128]{3,2,1,0:T(8,128)}, u32[]{:S(2)}) copy-start(f32[64,2,8,128]{3,2,1,0:T(8,128)} %get-tuple-element.13) | copy-start | bytes 1572868
  72.6 1.1 copy-start.2
  82.7 1.0 copy-start.6
  83.8 0.9 copy-start.8
  83.8 0.9 copy-start.12
  83.8 0.9 copy-start.13
  83.8 1.1 copy-start.10
  84.7 1.0 copy-start.1
  139.6 1.5 copy-start.11
  141.9 1.0 copy-start.39
  142.8 1.2 copy-start.22
  142.8 1.2 copy-start.24
  142.9 1.2 copy-start.26
  142.9 1.2 copy-start.37
  144.1 1.7 %copy-start.4 = (f32[64,2,8,128]{3,2,1,0:T(8,128)S(1)}, f32[64,2,8,128]{3,2,1,0:T(8,128)}, u32[]{:S(2)}) copy-start(f32[64,2,8,128]{3,2,1,0:T(8,128)} %get-tuple-element.16) | copy-start | bytes 1572868
  147.5 7.7 %copy-start.9 = (f32[64,4,256]{2,0,1:T(8,128)S(1)}, f32[64,4,256]{2,0,1:T(8,128)}, u32[]{:S(2)}) copy-start(f32[64,4,256]{2,0,1:T(8,128)} %fusion.3) | copy-start | bytes 786436
  (10 other events, 6.8 us)

commit v5 on v4

--- a/solution.py
+++ b/solution.py
@@ -231,15 +231,16 @@
     for side in range(CORES):
         parents_ref[:, side] = gather_ref[0, side * plane : (side + 1) * plane, rank:]
     leaves, entries = source_ref.shape[0], source_ref.shape[2] // rank
-    lane = lax.broadcasted_iota(jnp.int32, (rank, row_ref.shape[1]), 1)
+    lane = lax.broadcasted_iota(jnp.int32, row_ref.shape, 1)
     for target in range(leaves):
         for entry in range(entries):
             at_0 = where_ref[0, target * entries + entry]
             at_1 = where_ref[1, target * entries + entry]
             low = gather_ref[0, at_0, :rank]
             high = gather_ref[1, at_1, :rank]
-            named = jnp.broadcast_to(gather_ref[1, at_1, rank : rank + 1], lane.shape)
+            named = gather_ref[1, at_1, rank:]
             named = jnp.sum(jnp.where(lane == leaf, named, 0.0), axis=1, keepdims=True)
+            named = jnp.concatenate([named] * (rank // lane.shape[0]), axis=0)
             both = jnp.where(named < 1.5, low, high)
             odd = (named == 1.0) | (named == 3.0)
             source_ref[target, :, entry * rank : (entry + 1) * rank] = jnp.where(

time: 157 us -> 160 us (1.019)
  Pallas kernels: 122 us -> 125 us
    pallas_call x2, Pallas kernels: 109 us -> 112 us  [exchange(): pl.pallas_call(functools.partial(exchange_kernel, subs, leaf_total), out_...]
where the time goes in v5:
time: 160 us; the launch traced here: 159 us
  Pallas kernels  125 us (78%)
  matrix products  14 us (9%)
  local copies, waits for them, and re-layouts  12.9 us (8%)
  other arithmetic  6.09 us (4%)
    pallas_call x2, Pallas kernels, exchange(): pl.pallas_call(functools.partial(exchange_kernel, subs, leaf_total), out_...  112 us
    pallas_call x2, Pallas kernels, sum_over_sub(): pl.pallas_call(functools.partial(sum_kernel, subs), out_shape=jax.ShapeDt...  13.2 us
    dot_general x6, matrix products, one_product(): jnp.einsum('plb,lba->pla', padded[:, side:side + leaves], near_kernels[si...  7.73 us
    unnamed x91, local copies, waits for them, and re-layouts  5.42 us

profile of v5, /device:TPU:1, one launch (start us, length us, event | category | flops | bytes accessed | tf_op | source)
XLA Modules:
  0.0 159.2 jit_solution(14165283181203372756)
XLA Ops:
  0.0 0.7 copy-done.35
  2.4 1.3 fusion.115
  4.1 0.7 pad_maximum_fusion.11.parts_ref
  4.8 0.7 pad_maximum_fusion.9.skeleton_ref
  5.5 0.7 fusion.82.edges_ref
  6.2 61.2 %exchange.2 = (f32[4,64,512]{2,1,0:T(8,128)}, f32[64,2,8,128]{3,2,1,0:T(8,128)}, f32[2,72,256]{2,1,0:T(8,128)}) custom-call(f32[2,64,128]{2,1,0:T(8,128)} %pad_maximum_fusion.9.skeleton_ref, f32[8,128]{1,0:T(8,128)} %broadcast_in_dim.36.row_ref, f32[4,8,128]{2,1,0:T(8,128)} %pad_maximum_fusion.11.parts_ref, f32[2,72,256]{2,1,0:T(8,128)} %fusion.82.edges_ref, ...), custom_call_target="tpu_custom_call" | custom-call | tf_op jit(solution)/shard_map/exchange/pallas_call | solution.py:260
  67.4 0.7 slice_bitcast_fusion.10
  68.1 0.9 slice_bitcast_fusion.6
  69.6 1.0 fusion.8
  70.6 1.3 convolution_add_fusion.3
  72.0 1.7 %fusion.4 = f32[64,4,256]{2,0,1:T(8,128)} fusion(f32[4,256,64]{1,2,0:T(8,128)S(1)} %convolution_add_fusion.3, f32[4,256]{1,0:T(4,128)S(1)} %get-tuple-element.65, f32[4,256]{1,0:T(4,128)S(1)} %get-tuple-element.66, f32[4,256]{1,0:T(4,128)S(1)} %get-tuple-element.67, f32[4,256]{1,0:T(4,128)S(1)} %sub.147, f32[4,256]{1,0:T(4,128)S(1)} %sub.142, ...), kind=kOutput, calls=%fused_computation.10 | convolution fusion | flops 103677952 | bytes 876548 | tf_op jit(solution)/shard_map/plb,lba->pla/dot_general | solution.py:368
  74.3 0.8 copy-done.2
  75.5 0.7 pad_maximum_fusion.12.in_ref
  76.2 6.6 %sum_over_sub.2 = f32[32,128]{1,0:T(8,128)} custom-call(f32[32,128]{1,0:T(8,128)} %pad_maximum_fusion.12.in_ref), custom_call_target="tpu_custom_call" | custom-call | tf_op jit(solution)/shard_map/sum_over_sub/pallas_call | solution.py:318
  82.8 1.5 fusion.126
  84.2 0.6 gather_fusion
  86.4 0.8 copy-done.1
  87.7 0.9 convolution_bitcast_fusion.5
  88.6 0.8 copy.26
  89.4 0.7 pad_maximum_fusion.13.parts_ref
  90.1 0.7 pad_maximum_fusion.10.skeleton_ref
  90.8 0.7 fusion.81.edges_ref
  91.5 51.1 %exchange.3 = (f32[4,64,512]{2,1,0:T(8,128)}, f32[64,2,8,128]{3,2,1,0:T(8,128)}, f32[2,72,256]{2,1,0:T(8,128)}) custom-call(f32[2,64,128]{2,1,0:T(8,128)} %pad_maximum_fusion.10.skeleton_ref, f32[8,128]{1,0:T(8,128)} %broadcast_in_dim.36.row_ref, f32[4,8,128]{2,1,0:T(8,128)} %pad_maximum_fusion.13.parts_ref, f32[2,72,256]{2,1,0:T(8,128)} %fusion.81.edges_ref, ...), custom_call_target="tpu_custom_call" | custom-call | tf_op jit(solution)/shard_map/exchange/pallas_call | solution.py:260
  142.6 1.5 fusion.129
  144.2 0.6 copy-done.16
  144.9 1.0 fusion.7
  145.9 1.2 convolution_add_fusion.1
  147.1 1.7 %fusion.3 = f32[64,4,256]{2,0,1:T(8,128)} fusion(f32[4,256,64]{1,2,0:T(8,128)S(1)} %convolution_add_fusion.1, f32[4,256]{1,0:T(4,128)S(1)} %copy-done.24, f32[4,256]{1,0:T(4,128)S(1)} %copy-done.26, f32[4,256]{1,0:T(4,128)S(1)} %copy-done.22, f32[4,256]{1,0:T(4,128)S(1)} %copy-done.18, f32[4,256]{1,0:T(4,128)S(1)} %copy-done.20, ...), kind=kOutput, calls=%fused_computation.7 | convolution fusion | flops 103677952 | bytes 876548 | tf_op jit(solution)/shard_map/plb,lba->pla/dot_general | solution.py:368
  149.8 0.7 pad_maximum_fusion.14.in_ref
  150.5 6.6 %sum_over_sub.3 = f32[32,128]{1,0:T(8,128)} custom-call(f32[32,128]{1,0:T(8,128)} %pad_maximum_fusion.14.in_ref), custom_call_target="tpu_custom_call" | custom-call | tf_op jit(solution)/shard_map/sum_over_sub/pallas_call | solution.py:318
  157.1 0.9 fusion.125
  158.5 0.7 copy.41
  (127 shorter events, 7.1 us)
Async XLA Ops:
  0.0 84.2 %copy-start = (f32[32,64,64]{2,1,0:T(8,128)S(1)}, f32[32,64,64]{2,1,0:T(8,128)}, u32[]{:S(2)}) copy-start(f32[32,64,64]{2,1,0:T(8,128)} %param.15) | copy-start | bytes 1572868
  0.0 0.8 copy-start.33
  0.7 68.4 %copy-start.40 = (pred[4]{0:T(512)(128)(4,1)}, pred[4]{0:T(512)(128)(4,1)S(1)}, u32[]{:S(2)}) copy-start(pred[4]{0:T(512)(128)(4,1)S(1)} %compare_and_fusion.2) | copy-start | bytes 16
  0.9 69.7 %copy-start.38 = (pred[4]{0:T(512)(128)(4,1)}, pred[4]{0:T(512)(128)(4,1)S(1)}, u32[]{:S(2)}) copy-start(pred[4]{0:T(512)(128)(4,1)S(1)} %get-tuple-element.72) | copy-start | bytes 16
  0.9 71.1 %copy-start.36 = (pred[4]{0:T(512)(128)(4,1)}, pred[4]{0:T(512)(128)(4,1)S(1)}, u32[]{:S(2)}) copy-start(pred[4]{0:T(512)(128)(4,1)S(1)} %get-tuple-element.71) | copy-start | bytes 16
  0.9 1.4 copy-start.14
  2.3 69.6 %copy-start.15 = (f32[4,256]{1,0:T(4,128)}, f32[4,256]{1,0:T(4,128)S(1)}, u32[]{:S(2)}) copy-start(f32[4,256]{1,0:T(4,128)S(1)} %sub.137) | copy-start | bytes 12292
  2.3 69.6 %copy-start.17 = (f32[4,256]{1,0:T(4,128)}, f32[4,256]{1,0:T(4,128)S(1)}, u32[]{:S(2)}) copy-start(f32[4,256]{1,0:T(4,128)S(1)} %sub.147) | copy-start | bytes 12292
  2.4 69.6 %copy-start.19 = (f32[4,256]{1,0:T(4,128)}, f32[4,256]{1,0:T(4,128)S(1)}, u32[]{:S(2)}) copy-start(f32[4,256]{1,0:T(4,128)S(1)} %sub.142) | copy-start | bytes 12292
  2.4 1.3 copy-start.7
  4.1 1.4 copy-start.5
  69.0 3.0 %copy-start.21 = (f32[4,256]{1,0:T(4,128)}, f32[4,256]{1,0:T(4,128)S(1)}, u32[]{:S(2)}) copy-start(f32[4,256]{1,0:T(4,128)S(1)} %get-tuple-element.67) | copy-start | bytes 12292
  69.1 2.9 %copy-start.23 = (f32[4,256]{1,0:T(4,128)}, f32[4,256]{1,0:T(4,128)S(1)}, u32[]{:S(2)}) copy-start(f32[4,256]{1,0:T(4,128)S(1)} %get-tuple-element.65) | copy-start | bytes 12292
  69.1 2.9 %copy-start.25 = (f32[4,256]{1,0:T(4,128)}, f32[4,256]{1,0:T(4,128)S(1)}, u32[]{:S(2)}) copy-start(f32[4,256]{1,0:T(4,128)S(1)} %get-tuple-element.66) | copy-start | bytes 12292
  69.1 1.5 copy-start.29
  69.1 1.5 copy-start.31
  72.0 1.7 %copy-start.3 = (f32[64,2,8,128]{3,2,1,0:T(8,128)S(1)}, f32[64,2,8,128]{3,2,1,0:T(8,128)}, u32[]{:S(2)}) copy-start(f32[64,2,8,128]{3,2,1,0:T(8,128)} %get-tuple-element.13) | copy-start | bytes 1572868
  74.1 1.1 copy-start.2
  84.2 1.0 copy-start.6
  85.3 0.9 copy-start.8
  85.3 0.9 copy-start.12
  85.3 0.9 copy-start.13
  85.3 1.1 copy-start.10
  86.2 1.0 copy-start.1
  142.6 1.5 copy-start.11
  144.9 1.0 copy-start.39
  145.9 1.2 copy-start.22
  145.9 1.2 copy-start.24
  145.9 1.2 copy-start.26
  145.9 1.2 copy-start.37
  147.1 1.7 %copy-start.4 = (f32[64,2,8,128]{3,2,1,0:T(8,128)S(1)}, f32[64,2,8,128]{3,2,1,0:T(8,128)}, u32[]{:S(2)}) copy-start(f32[64,2,8,128]{3,2,1,0:T(8,128)} %get-tuple-element.16) | copy-start | bytes 1572868
  150.5 7.7 %copy-start.9 = (f32[64,4,256]{2,0,1:T(8,128)S(1)}, f32[64,4,256]{2,0,1:T(8,128)}, u32[]{:S(2)}) copy-start(f32[64,4,256]{2,0,1:T(8,128)} %fusion.3) | copy-start | bytes 786436
  (10 other events, 6.8 us)
